TPU v7x, 128 devices: a whole 4x4x4 slice. The times are simulated.
128 devices in a mesh: section: 4 (over x), ctx: 32 (over y, z, core).
Axes of the slice: x: 4, y: 4, z: 4, core: 2. Of those that a mesh axis runs over, the one named last changes fastest.
Arguments:
- resid: bfloat16 [4, 4096, 6144], P('section', 'ctx'), may hold values from -6 to 6
- queries: bfloat16 [4, 4096, 6144], P('section', 'ctx'), may hold values from -6 to 6
- keys: bfloat16 [4, 4096, 6144], P('section', 'ctx'), may hold values from -6 to 6
- values: bfloat16 [4, 4096, 6144], P('section', 'ctx'), may hold values from -6 to 6
- log_decay: float32 [4, 4096, 48], P('section', 'ctx'), may hold values from -3 to 0
- attn_gain: float32 [4, 6144], P('section'), may hold values from 0.25 to 1.75
- moe_gain: float32 [4, 6144], P('section'), may hold values from 0.25 to 1.75
- experts: int32 [4, 4096, 2], P('section', 'ctx'), may hold values from 0 to 31, all different within a row; in each aligned block of 128 rows (0 to 127, 128 to 255, ..., all dimensions but the last counted through in order) at most 16 rows name the same one
- combine_weight: float32 [4, 4096, 2], P('section', 'ctx'), may hold values from 0.2 to 1
- w_up: bfloat16 [4, 6144, 20480], P('section', None, 'ctx'), may hold values from -0.078125 to 0.078125
- w_down: bfloat16 [4, 20480, 6144], P('section', 'ctx'), may hold values from -0.078125 to 0.078125
Outputs:
- received: bfloat16 [4, 4096, 6144], P('section', 'ctx')
Inputs may be any that keep to these rules, and one draw needn't show every extreme that they name: In the rows of one device each expert is named at most 16 times, and the two experts of a token differ.
All inputs are finite; a program needn't handle non-finite values.
Results may differ from a plain program's by a relative error of at most 0.002.
Values may be sent and summed in bfloat16 or wider, within the bound.
A program may use at most 256 MiB of HBM per device.

v0:
```python
import jax
import jax.numpy as jnp
from jax import lax
from jax.sharding import PartitionSpec as P

D = 6144
LINEAR_HEADS = 48
HEAD = 128
EXPERTS = 32
SHARDS = 8
CAP_SRC = 16


HIGH = lax.Precision.HIGHEST


def prefix_2(part, axis, combine, identity):
    place = lax.axis_index(axis)
    gathered = jax.tree.map(lambda a: lax.all_gather(a, axis), part)
    state = jax.tree.map(lambda a, e: jnp.zeros_like(a) + jnp.asarray(e, a.dtype), part, identity)

    def one(step, state):
        return combine(
            state, jax.tree.map(lambda a: lax.dynamic_index_in_dim(a, step, 0, False), gathered)
        )

    return lax.fori_loop(0, place, one, state)


def passed_along(value, axis, steps):
    count = lax.axis_size(axis)
    pairs = [(source, (source + steps) % count) for source in range(count)]
    return lax.ppermute(value, axis, pairs)


def rms_scale(values_in, gain):
    return (
        values_in
        * lax.rsqrt(jnp.mean(values_in * values_in, axis=-1, keepdims=True) + 1e-06)
        * gain
    )


def slots_of(chosen):
    onehot = (chosen[:, None] == jnp.arange(EXPERTS)[None, :]).astype(jnp.int32)
    before = jnp.cumsum(onehot, axis=0) - onehot
    return jnp.sum(before * onehot, axis=1)


def join_states(earlier, later):
    return (earlier[0] * later[0], later[0][:, None, None] * earlier[1] + later[1])


def local(
    resid,
    queries,
    keys,
    values,
    log_decay,
    attn_gain,
    moe_gain,
    experts,
    combine_weight,
    w_up,
    w_down,
):
    length = queries.shape[1]
    query = queries[0].astype(jnp.float32).reshape(length, LINEAR_HEADS, HEAD)
    keyrows = keys[0].astype(jnp.float32).reshape(length, LINEAR_HEADS, HEAD)
    valrows = values[0].astype(jnp.float32).reshape(length, LINEAR_HEADS, HEAD)
    log_rate = log_decay[0]
    cumul = jnp.cumsum(log_rate, axis=0)
    scores = jnp.einsum("thd,shd->hts", query, keyrows, precision=HIGH)
    spread = cumul.T[:, :, None] - cumul.T[:, None, :]
    lower = jnp.arange(length)[:, None] >= jnp.arange(length)[None, :]
    weights = jnp.exp(jnp.where(lower[None], spread, -1e30))
    intra = jnp.einsum("hts,shd->thd", scores * weights, valrows, precision=HIGH)
    tail_decay = jnp.exp(cumul[-1][None, :] - cumul)
    state = jnp.einsum("thd,the->hde", keyrows * tail_decay[:, :, None], valrows, precision=HIGH)
    identity = (
        jnp.ones((LINEAR_HEADS,), jnp.float32),
        jnp.zeros((LINEAR_HEADS, HEAD, HEAD), jnp.float32),
    )
    prefix = prefix_2((jnp.exp(cumul[-1]), state), "ctx", join_states, identity)
    inter = jnp.exp(cumul)[:, :, None] * jnp.einsum(
        "thd,hde->the", query, prefix[1], precision=HIGH
    )
    attn_raw = (intra + inter).reshape(length, D)
    hres = resid[0].astype(jnp.float32) + rms_scale(attn_raw, attn_gain[0])
    normed = rms_scale(hres, moe_gain[0]).astype(jnp.bfloat16)
    ctx_count = lax.axis_size("ctx")
    flying = ctx_count // SHARDS
    my_expert = lax.axis_index("ctx") // SHARDS
    chosen = experts[0].reshape(-1)
    slot = slots_of(chosen)
    target = chosen * CAP_SRC + slot
    in_window = chosen < flying
    select = (
        (target[None, :] == jnp.arange(flying * CAP_SRC)[:, None]) & in_window[None, :]
    ).astype(jnp.bfloat16)
    doubled = jnp.repeat(normed, 2, axis=0)
    outbox = jnp.dot(select, doubled, preferred_element_type=jnp.float32).astype(jnp.bfloat16)
    outbox = outbox.reshape(flying, CAP_SRC, D)
    up_local = w_up[0]
    down_local = w_down[0]
    mine = lax.dynamic_index_in_dim(
        lax.all_gather(outbox[None], "ctx", axis=0, tiled=True), my_expert, 1, False
    )
    count = mine.shape[0]
    hidden = jax.nn.gelu(
        jnp.dot(mine.reshape(count * CAP_SRC, D), up_local, preferred_element_type=jnp.float32),
        approximate=True,
    ).astype(jnp.bfloat16)
    partial_value = (
        jnp.dot(hidden, down_local, preferred_element_type=jnp.float32)
        .astype(jnp.bfloat16)
        .reshape(count, CAP_SRC, D)
    )
    returned = lax.all_to_all(partial_value, "ctx", split_axis=0, concat_axis=0, tiled=True)
    summed = returned.reshape(flying, SHARDS, CAP_SRC, D).astype(jnp.float32).sum(axis=1)
    summed = summed.reshape(flying * CAP_SRC, D)
    picked = jnp.take(summed, jnp.clip(target, 0, flying * CAP_SRC - 1), axis=0)
    picked = jnp.where(in_window[:, None], picked, 0.0) * combine_weight[0].reshape(-1)[:, None]
    mixed = picked.reshape(length, 2, D).sum(axis=1)
    layer_out = (hres + mixed).astype(jnp.bfloat16)
    return passed_along(layer_out[None], "section", 1)


def solution(mesh):
    return jax.shard_map(
        local,
        mesh=mesh,
        in_specs=(
            P("section", "ctx", None),
            P("section", "ctx", None),
            P("section", "ctx", None),
            P("section", "ctx", None),
            P("section", "ctx", None),
            P("section", None),
            P("section", None),
            P("section", "ctx", None),
            P("section", "ctx", None),
            P("section", None, "ctx"),
            P("section", "ctx", None),
        ),
        out_specs=P("section", "ctx", None),
        check_vma=False,
    )
```

profile of v0, /device:TPU:0, one launch (start us, length us, event | category | flops | bytes accessed | tf_op | source)
XLA Modules:
  0.0 699.7 jit_solution(13463973919009002502)
XLA Ops:
  6.5 0.9 copy.47
  7.8 1.9 copy.66
  10.1 1.1 copy-done.2
  11.2 3.5 fusion.7
  15.9 1.8 copy.68
  17.8 0.6 reduce-window.6
  18.6 23.0 %all-gather.1 = f32[32,1,48]{2,1,0:T(1,128)S(1)} all-gather(f32[1,1,48]{2,1,0:T(1,128)S(1)} %get-tuple-element.63), channel_id=1, replica_groups=mesh['section'=4,'ctx'=32] {'ctx'}, dimensions={0}, use_global_device_ids=true | all-gather | bytes 6336 | tf_op jit(solution)/shard_map/all_gather | solution.py:19
  42.3 0.8 copy-done.3
  43.2 5.5 fusion.10
  48.7 257.2 %all-gather.7.cloned.1.call-done = f32[1536,128,128]{2,1,0:T(8,128)} async-done(((f32[48,128,128]{2,1,0:T(8,128)}), f32[1536,128,128]{2,1,0:T(8,128)}) %all-gather.7.cloned.1.call-update) | async-done | bytes 100663312 | tf_op jit(solution)/shard_map/all_gather | solution.py:19
  306.3 6.6 multiply_reduce_fusion.2
  312.9 2.4 copy.63
  315.4 2.3 multiply_reduce_fusion.1
  317.7 1.9 multiply_convert_fusion
  319.6 4.9 broadcast_in_dim.63
  324.5 6.2 reshape.247
  330.7 1.5 convolution_convert_fusion.1
  332.3 168.0 %all-gather.5.cloned.1.call-done = bf16[32,4,16,6144]{3,2,1,0:T(8,128)(2,1)} async-done(((bf16[1,4,16,6144]{3,2,1,0:T(8,128)(2,1)}), bf16[32,4,16,6144]{3,2,1,0:T(8,128)(2,1)}) %all-gather.5.cloned.1.call-update) | async-done | bytes 25165840 | tf_op jit(solution)/shard_map/all_gather | solution.py:107
  500.3 3.3 constant_dynamic-slice_fusion
  503.7 8.6 %fusion.34 = bf16[512,640]{1,0:T(8,128)(2,1)S(1)} fusion(bf16[512,6144]{1,0:T(8,128)(2,1)S(1)} %bitcast.107, bf16[1,6144,640]{2,1,0:T(8,128)(2,1)} %param.22), kind=kOutput, calls=%fused_computation.46 | convolution fusion | flops 4029480960 | bytes 14811136 | tf_op jit(solution)/shard_map/dot_general | solution.py:111
  512.3 7.1 %convolution_convert_fusion = bf16[512,6144]{1,0:T(8,128)(2,1)} fusion(bf16[512,640]{1,0:T(8,128)(2,1)S(1)} %fusion.34, bf16[1,640,6144]{2,1,0:T(8,128)(2,1)S(1)} %bitcast.122), kind=kOutput, calls=%fused_computation.4 | convolution fusion | flops 4029677568 | bytes 14811136 | tf_op jit(solution)/shard_map/dot_general | solution.py:115
  519.4 5.9 all-to-all-start
  525.9 2.4 copy.57
  528.3 76.9 %all-to-all-done = bf16[32,16,6144]{2,1,0:T(8,128)(2,1)} async-done(((bf16[32,16,6144]{2,1,0:T(8,128)(2,1)}), bf16[32,16,6144]{2,1,0:T(8,128)(2,1)}, u32[]{:S(2)}, u32[]{:S(2)}) %all-to-all-start) | async-done | bytes 6291488 | tf_op jit(solution)/shard_map/all_to_all | solution.py:119
  605.3 4.0 convert_reduce_fusion
  609.3 5.1 gather_fusion
  614.4 8.1 %gather.7 = f32[128,2,6144]{2,1,0:T(2,128)} reshape(f32[256,6144]{1,0:T(8,128)} %gather_fusion) | data formatting | bytes 12582912 | tf_op jit(solution)/shard_map/jit(_take)/gather | solution.py:122
  622.6 32.9 %multiply_reduce_fusion = f32[128,6144]{1,0:T(8,128)S(1)} fusion(f32[128,2,6144]{2,1,0:T(2,128)} %gather.7, pred[128,2]{1,0:T(8,128)(4,1)S(1)} %compare_and_fusion, pred[128,2]{1,0:T(8,128)(4,1)S(1)} %copy.58, f32[128,2]{1,0:T(8,128)S(1)} %copy.64), kind=kLoop, calls=%fused_computation.9 | loop fusion | flops 5505024 | bytes 9438720 | tf_op jit(solution)/shard_map/reduce_sum | solution.py:124
  655.5 0.7 fusion.4
  656.2 1.5 collective-permute-start
  657.7 34.0 %collective-permute-done = bf16[1,128,6144]{2,1,0:T(8,128)(2,1)S(1)} collective-permute-done((bf16[1,128,6144]{2,1,0:T(8,128)(2,1)S(1)}, bf16[1,128,6144]{2,1,0:T(8,128)(2,1)S(1)}, u32[]{:S(2)}, u32[]{:S(2)}) %collective-permute-start) | collective-permute-done | bytes 1572896 | tf_op jit(solution)/shard_map/ppermute | solution.py:33
  691.7 1.1 copy.88
  (63 shorter events, 3.8 us)
Async XLA Ops:
  6.5 3.2 copy-start.7
  6.5 299.3 %all-gather.7.cloned.1.call-start = ((), (), s32[]{:S(2)}) async-start(), calls=%async_computation.2 | async-start | bytes 103809024 | tf_op jit(solution)/shard_map/all_gather | solution.py:19
  10.1 1.2 copy-start.2
  14.8 0.7 copy-start.11
  14.8 485.5 %all-gather.5.cloned.1.call-start = ((), (), s32[]{:S(2)}) async-start(), calls=%async_computation.1 | async-start | bytes 25952256 | tf_op jit(solution)/shard_map/all_gather | solution.py:107
  17.7 24.7 %copy-start.1 = (bf16[16,8,48,128]{3,2,1,0:T(8,128)(2,1)}, bf16[16,8,48,128]{3,2,1,0:T(8,128)(2,1)S(1)}, u32[]{:S(2)}) copy-start(bf16[16,8,48,128]{3,2,1,0:T(8,128)(2,1)S(1)} %copy.68) | copy-start | bytes 4718596
  41.7 1.4 copy-start.3
  312.9 2.4 copy-start.8
  315.3 2.4 copy-start.4
  315.3 2.3 copy-start.9
  500.3 12.0 %slice-start = ((s8[7864320]{0:T(1024)(128)(4,1)}), s8[4194304]{0:T(1024)(128)(4,1)S(1)}, s32[]{:S(2)}) async-start(s8[7864320]{0:T(1024)(128)(4,1)} %bitcast.121), calls=%async_computation.3 | async-start | bytes 8388608
  503.6 8.6 %slice-start.1 = ((s8[7864320]{0:T(1024)(128)(4,1)}), s8[3670016]{0:T(1024)(128)(4,1)S(1)}, s32[]{:S(2)}) async-start(s8[7864320]{0:T(1024)(128)(4,1)} %bitcast.121), calls=%async_computation.4 | async-start | bytes 7340032
  519.4 6.2 copy-start.10
  519.4 6.6 copy-start
  519.4 85.9 %all-to-all-start = ((bf16[32,16,6144]{2,1,0:T(8,128)(2,1)}), bf16[32,16,6144]{2,1,0:T(8,128)(2,1)}, u32[]{:S(2)}, u32[]{:S(2)}) async-start(bf16[32,16,6144]{2,1,0:T(8,128)(2,1)} %bitcast.106), calls=%async_computation | async-start | bytes 12582912 | tf_op jit(solution)/shard_map/all_to_all | solution.py:119
  622.6 32.9 %copy-start.5 = (bf16[1,128,6144]{2,1,0:T(8,128)(2,1)S(1)}, bf16[1,128,6144]{2,1,0:T(8,128)(2,1)}, u32[]{:S(2)}) copy-start(bf16[1,128,6144]{2,1,0:T(8,128)(2,1)} %param.13) | copy-start | bytes 4718596
  622.6 32.9 %copy-start.6 = (f32[1,128,6144]{2,1,0:T(8,128)S(1)}, f32[1,128,6144]{2,1,0:T(8,128)}, u32[]{:S(2)}) copy-start(f32[1,128,6144]{2,1,0:T(8,128)} %copy.57) | copy-start | bytes 9437188
  656.2 35.5 %collective-permute-start = (bf16[1,128,6144]{2,1,0:T(8,128)(2,1)S(1)}, bf16[1,128,6144]{2,1,0:T(8,128)(2,1)S(1)}, u32[]{:S(2)}, u32[]{:S(2)}) collective-permute-start(bf16[1,128,6144]{2,1,0:T(8,128)(2,1)S(1)} %fusion.4), channel_id=1, source_target_pairs={{0,32},{32,64},{64,96},{96,0},{1,33},{33,65},{65,97},{97,1},{2,34}... | collective-permute-start | bytes 4718600 | tf_op jit(solution)/shard_map/ppermute | solution.py:33
Sparse Core Ops, SparseCore 0:
  14.9 290.9 all-gather.6
  332.4 167.8 all-gather.4
where the time goes:
time: 711 us; the launch traced here: 700 us
  waiting for transfers between devices  536 us (75%)
  local copies, waits for them, and re-layouts  43 us (6%)
  other arithmetic  42.9 us (6%)
  matrix products  33.5 us (5%)
  blocking collectives  23 us (3%)
  between operations  13.8 us (2%)
  starting transfers between devices  7.49 us (1%)
    all_gather x1, waiting for transfers between devices, prefix_2(): gathered = jax.tree.map(lambda a: lax.all_gather(a, axis), part)  257 us
    all_gather x1, waiting for transfers between devices, local(): lax.all_gather(outbox[None], 'ctx', axis=0, tiled=True)  168 us
    all_to_all x1, waiting for transfers between devices, local(): lax.all_to_all(partial_value, 'ctx', split_axis=0, concat_axis=0, tiled=T...  76.9 us
    ppermute x1, waiting for transfers between devices, passed_along(): return lax.ppermute(value, axis, pairs)  34 us
    reduce_sum x1, other arithmetic, local(): mixed = picked.reshape(length, 2, D).sum(axis=1)  32.9 us
    all_gather x1, blocking collectives, prefix_2(): gathered = jax.tree.map(lambda a: lax.all_gather(a, axis), part)  23 us
  transfers between devices with their start and end apart: 4, of which 4 were waited for; matrix products, arithmetic and copies ran while one was open for 2% of the time, Pallas kernels for 0%

commit v1 on v0

v1 whole, which is shorter than its diff:
```python
import jax
import jax.numpy as jnp
from jax import lax
from jax.experimental import pallas as pl
from jax.experimental.pallas import tpu as pltpu
from jax.sharding import PartitionSpec as P

D = 6144
HEADS = 48
HEAD = 128
TOK = 128
EXPERTS = 32
SHARDS = 8
CAP = 16
FLY = 4
GROUP = 6
ROWS = GROUP * HEAD
MESSAGE = ROWS + 8
BF = jnp.bfloat16
F32 = jnp.float32
HIGH = lax.Precision.HIGHEST


def dot(a, b):
    return jnp.dot(a, b, preferred_element_type=F32)


def dot_t(a, b):
    return lax.dot_general(a, b, (((1,), (1,)), ((), ())), preferred_element_type=F32)


def parts(x):
    high = x.astype(BF)
    return high, (x - high.astype(F32)).astype(BF)


def place():
    me = lax.axis_index("ctx")
    return me // 8, lax.rem(me // 2, 4), lax.rem(me, 2)


def index_of(y, z, c):
    return (y * 4 + z) * 2 + c


def columns(h):
    return pl.ds(pl.multiple_of(h * HEAD, HEAD), HEAD)


def attention_kernel(
    q_hbm, k_hbm, v_hbm, resid_hbm, rate_ref, attn_gain_ref, moe_gain_ref, select_ref,
    hres_ref, outbox_ref,
    q_ref, k_ref, v_ref, resid_ref, cum_ref, total_ref, partner_total, own_state,
    partner_state, t_send, t_recv, within, r_send, r_recv, p_send, chip_prefix,
    f_send, prefix, attn_ref, square_ref,
    load_sems, small_sems, ps_send_sems, ps_recv_sems, t_send_sems, t_recv_sems,
    r_send_sems, r_recv_sems, p_send_sems, p_recv_sems, f_send_sems, f_recv_sems,
):
    y, z, c = place()
    loads = [
        pltpu.make_async_copy(a, b, load_sems.at[i])
        for i, (a, b) in enumerate(
            ((k_hbm, k_ref), (v_hbm, v_ref), (q_hbm, q_ref), (resid_hbm, resid_ref))
        )
    ]
    for load in loads:
        load.start()
    barrier = pltpu.get_barrier_semaphore()
    partner = index_of(y, z, 1 - c)
    z_peer = [index_of(y, lax.rem(z + d, 4), c) for d in range(4)]
    y_peer = [index_of(lax.rem(y + d, 4), z, c) for d in range(4)]
    for peer in [partner] + z_peer[1:] + y_peer[1:]:
        pl.semaphore_signal(barrier, inc=1, device_id={"ctx": peer})

    rate = rate_ref[...]
    earlier = lax.broadcasted_iota(jnp.int32, (TOK, TOK), 0)
    later = lax.broadcasted_iota(jnp.int32, (TOK, TOK), 1)
    cum_ref[...] = jnp.dot(
        rate, (earlier <= later).astype(F32), precision=HIGH, preferred_element_type=F32
    )
    total_ref[...] = jnp.dot(
        rate, jnp.ones((TOK, TOK), F32), precision=HIGH, preferred_element_type=F32
    )
    pl.semaphore_wait(barrier, 7)

    def remote(src, dst, send, recv, peer):
        copy = pltpu.make_async_remote_copy(
            src_ref=src, dst_ref=dst, send_sem=send, recv_sem=recv, device_id={"ctx": peer}
        )
        return copy

    started = []
    totals = remote(total_ref, partner_total, small_sems.at[0], small_sems.at[1], partner)
    totals.start()
    loads[0].wait()
    loads[1].wait()

    def state_of(h):
        row = jnp.exp(total_ref[pl.ds(h, 1), :] - cum_ref[pl.ds(h, 1), :])
        keys = k_ref[:, columns(h)].astype(F32).T * row
        high, low = parts(keys)
        values = v_ref[:, columns(h)]
        return dot(high, values) + dot(low, values)

    order = (2, 1, 3, 0)
    ps_copies = {}
    for d in order:
        j = lax.rem(z + d, 4)

        def one(i, carry, j=j):
            h = (1 - c) * 24 + j * GROUP + i
            own_state[1 - c, j, pl.ds(pl.multiple_of(i * HEAD, HEAD), HEAD), :] = state_of(h)
            return carry

        lax.fori_loop(0, GROUP, one, 0)
        copy = remote(
            own_state.at[1 - c, j], partner_state.at[j], ps_send_sems.at[d], ps_recv_sems.at[d], partner
        )
        copy.start()
        ps_copies[d] = copy
    totals.wait()

    zero_first = c == 0
    t_copies = {}
    for d in order:
        j = lax.rem(z + d, 4)

        def one(i, carry, j=j):
            h = c * 24 + j * GROUP + i
            own_state[c, j, pl.ds(pl.multiple_of(i * HEAD, HEAD), HEAD), :] = state_of(h)
            return carry

        lax.fori_loop(0, GROUP, one, 0)
        ps_copies[d].wait_recv()
        target = t_recv.at[0] if d == 0 else t_send.at[d - 1]

        def join(i, carry, j=j, target=target):
            h = c * 24 + j * GROUP + i
            mine = total_ref[pl.ds(h, 1), :]
            other = partner_total[pl.ds(h, 1), :]
            keep = jnp.exp(jnp.where(zero_first, other, 0.0))
            take = jnp.exp(jnp.where(zero_first, 0.0, mine))
            rows = pl.ds(pl.multiple_of(i * HEAD, HEAD), HEAD)
            target[rows, :] = keep * own_state[c, j, rows, :] + take * partner_state[j, rows, :]
            target[pl.ds(ROWS + i, 1), :] = mine + other
            return carry

        lax.fori_loop(0, GROUP, join, 0)
        target[ROWS + GROUP :, :] = jnp.zeros((8 - GROUP, HEAD), F32)
        if d:
            copy = remote(
                target, t_recv.at[d], t_send_sems.at[d - 1], t_recv_sems.at[d - 1], z_peer[d]
            )
            copy.start()
            t_copies[d] = copy

    loads[2].wait()
    lower = earlier >= later

    def intra(h, carry):
        cum = cum_ref[pl.ds(h, 1), :]
        across = jnp.broadcast_to(cum, (TOK, TOK))
        weights = jnp.exp(jnp.where(lower, across.T - across, -1e30))
        scores = dot_t(q_ref[:, columns(h)], k_ref[:, columns(h)]) * weights
        high, low = parts(scores)
        values = v_ref[:, columns(h)]
        attn_ref[:, columns(h)] = dot(high, values) + dot(low, values)
        return carry

    lax.fori_loop(0, 18, intra, 0)

    for d in (1, 3, 2):
        t_copies[d].wait_recv()

    def row_sum(i, carry):
        rows = pl.ds(pl.multiple_of(i * HEAD, HEAD), HEAD)
        label = pl.ds(ROWS + i, 1)
        state = t_recv[z, rows, :]
        within[1, rows, :] = state
        for other in range(1, 4):
            slot = lax.rem(z - other + 4, 4)
            state = state * jnp.exp(t_recv[slot, label, :]) + t_recv[slot, rows, :]
            if other < 3:
                within[other + 1, rows, :] = state
        r_send[rows, :] = state
        r_send[label, :] = (
            t_recv[0, label, :] + t_recv[1, label, :] + t_recv[2, label, :] + t_recv[3, label, :]
        )
        return carry

    lax.fori_loop(0, GROUP, row_sum, 0)
    r_send[ROWS + GROUP :, :] = jnp.zeros((8 - GROUP, HEAD), F32)
    r_copies = {}
    for d in (2, 1, 3):
        copy = remote(r_send, r_recv.at[d], r_send_sems.at[d - 1], r_recv_sems.at[d - 1], y_peer[d])
        copy.start()
        r_copies[d] = copy
    lax.fori_loop(18, 34, intra, 0)
    r_recv[0] = r_send[...]
    for d in (1, 3, 2):
        r_copies[d].wait_recv()

    def row_prefix(i, carry):
        rows = pl.ds(pl.multiple_of(i * HEAD, HEAD), HEAD)
        label = pl.ds(ROWS + i, 1)
        state = jnp.zeros((HEAD, HEAD), F32)
        for other in range(3):
            slot = lax.rem(y - other + 4, 4)
            joined = state * jnp.exp(r_recv[slot, label, :]) + r_recv[slot, rows, :]
            state = jnp.where(other < y, joined, state)
        within[0, rows, :] = state
        return carry

    lax.fori_loop(0, GROUP, row_prefix, 0)
    p_copies = {}
    for d in order:
        to = lax.rem(z + d, 4)
        target = chip_prefix.at[0] if d == 0 else p_send.at[d - 1]

        def chip(i, carry, to=to, target=target):
            rows = pl.ds(pl.multiple_of(i * HEAD, HEAD), HEAD)
            label = pl.ds(ROWS + i, 1)
            gone = jnp.zeros((1, HEAD), F32)
            for other in range(3):
                slot = lax.rem(z - other + 4, 4)
                gone = gone + jnp.where(other < to, t_recv[slot, label, :], 0.0)
            start = within[0, rows, :]
            target[rows, :] = start * jnp.exp(gone) + jnp.where(to > 0, within[jnp.maximum(to, 1), rows, :], 0.0)
            return carry

        lax.fori_loop(0, GROUP, chip, 0)
        if d:
            copy = remote(
                target, chip_prefix.at[d], p_send_sems.at[d - 1], p_recv_sems.at[d - 1], z_peer[d]
            )
            copy.start()
            p_copies[d] = copy
    lax.fori_loop(34, 48, intra, 0)

    f_copies = {}
    for d in (0, 1, 3, 2):
        if d:
            p_copies[d].wait_recv()
        j = lax.rem(z - d + 4, 4)

        def core(i, carry, d=d, j=j):
            h = c * 24 + j * GROUP + i
            rows = pl.ds(pl.multiple_of(i * HEAD, HEAD), HEAD)
            first_total = jnp.where(zero_first, total_ref[pl.ds(h, 1), :], partner_total[pl.ds(h, 1), :])
            first_state = jnp.where(zero_first, own_state[c, j, rows, :], partner_state[j, rows, :])
            base = chip_prefix[d, rows, :]
            full = base * jnp.exp(first_total) + first_state
            prefix[c, j, rows, :] = jnp.where(zero_first, base, full)
            f_send[j, rows, :] = jnp.where(zero_first, full, base)
            return carry

        lax.fori_loop(0, GROUP, core, 0)
        copy = remote(f_send.at[j], prefix.at[c, j], f_send_sems.at[d], f_recv_sems.at[d], partner)
        copy.start()
        f_copies[d] = copy

    square_ref[...] = jnp.zeros_like(square_ref)

    def inter(half, j):
        def one(i, carry):
            h = half * 24 + j * GROUP + i
            rows = pl.ds(pl.multiple_of(i * HEAD, HEAD), HEAD)
            across = jnp.broadcast_to(cum_ref[pl.ds(h, 1), :], (TOK, TOK)).T
            high, low = parts(prefix[half, j, rows, :])
            query = q_ref[:, columns(h)]
            out = attn_ref[:, columns(h)] + jnp.exp(across) * (dot(query, high) + dot(query, low))
            attn_ref[:, columns(h)] = out
            square_ref[...] += out * out
            return carry

        lax.fori_loop(0, GROUP, one, 0)

    for d in (0, 1, 3, 2):
        inter(c, lax.rem(z - d + 4, 4))
    for d in (0, 1, 3, 2):
        f_copies[d].wait_recv()
        inter(1 - c, lax.rem(z - d + 4, 4))
    loads[3].wait()
    scale = lax.rsqrt(jnp.sum(square_ref[...], axis=1, keepdims=True) * (1.0 / D) + 1e-6)
    scale = jnp.broadcast_to(scale, (TOK, HEAD))
    square_ref[...] = jnp.zeros_like(square_ref)

    def residual(h, carry):
        out = resid_ref[:, columns(h)].astype(F32) + attn_ref[:, columns(h)] * scale * attn_gain_ref[:, columns(h)]
        hres_ref[:, columns(h)] = out
        square_ref[...] += out * out
        return carry

    lax.fori_loop(0, HEADS, residual, 0)
    scale_2 = lax.rsqrt(jnp.sum(square_ref[...], axis=1, keepdims=True) * (1.0 / D) + 1e-6)
    scale_2 = jnp.broadcast_to(scale_2, (TOK, HEAD))
    select = select_ref[...]

    def norm(h, carry):
        normed = (hres_ref[:, columns(h)] * scale_2 * moe_gain_ref[:, columns(h)]).astype(BF)
        outbox_ref[:, columns(h)] = dot(select, normed).astype(BF)
        return carry

    lax.fori_loop(0, HEADS, norm, 0)
    for copies in (ps_copies, t_copies, r_copies, p_copies, f_copies):
        for copy in copies.values():
            copy.wait_send()


def attention(queries, keys, values, resid, rate, attn_gain, moe_gain, select):
    vmem = pl.BlockSpec(memory_space=pltpu.VMEM)
    hbm = pl.BlockSpec(memory_space=pl.ANY)
    dma = pltpu.SemaphoreType.DMA
    return pl.pallas_call(
        attention_kernel,
        out_shape=(
            jax.ShapeDtypeStruct((TOK, D), F32),
            jax.ShapeDtypeStruct((FLY * CAP, D), BF),
        ),
        in_specs=[hbm] * 4 + [vmem] * 4,
        out_specs=(vmem, vmem),
        scratch_shapes=[
            pltpu.VMEM((TOK, D), BF),
            pltpu.VMEM((TOK, D), BF),
            pltpu.VMEM((TOK, D), BF),
            pltpu.VMEM((TOK, D), BF),
            pltpu.VMEM((HEADS, TOK), F32),
            pltpu.VMEM((HEADS, TOK), F32),
            pltpu.VMEM((HEADS, TOK), F32),
            pltpu.VMEM((2, 4, ROWS, HEAD), F32),
            pltpu.VMEM((4, ROWS, HEAD), F32),
            pltpu.VMEM((3, MESSAGE, HEAD), F32),
            pltpu.VMEM((4, MESSAGE, HEAD), F32),
            pltpu.VMEM((4, ROWS, HEAD), F32),
            pltpu.VMEM((MESSAGE, HEAD), F32),
            pltpu.VMEM((4, MESSAGE, HEAD), F32),
            pltpu.VMEM((3, ROWS, HEAD), F32),
            pltpu.VMEM((4, ROWS, HEAD), F32),
            pltpu.VMEM((4, ROWS, HEAD), F32),
            pltpu.VMEM((2, 4, ROWS, HEAD), F32),
            pltpu.VMEM((TOK, D), F32),
            pltpu.VMEM((TOK, HEAD), F32),
            dma((4,)), dma((2,)), dma((4,)), dma((4,)), dma((3,)), dma((3,)),
            dma((3,)), dma((3,)), dma((3,)), dma((3,)), dma((4,)), dma((4,)),
        ],
        compiler_params=pltpu.CompilerParams(
            collective_id=0, has_side_effects=True, vmem_limit_bytes=56 * 2**20
        ),
        name="attention",
    )(queries, keys, values, resid, rate, attn_gain, moe_gain, select)


def slots_of(chosen):
    count = chosen.shape[0]
    onehot = (chosen[:, None] == jnp.arange(EXPERTS)[None, :]).astype(BF)
    before = (jnp.arange(count)[:, None] > jnp.arange(count)[None, :]).astype(BF)
    ahead = dot(before, onehot)
    return jnp.sum(ahead * onehot.astype(F32), axis=1).astype(jnp.int32)


def local(
    resid, queries, keys, values, log_decay, attn_gain, moe_gain, experts, combine_weight, w_up, w_down
):
    chosen = experts[0].reshape(-1)
    slot = slots_of(chosen)
    target = chosen * CAP + slot
    in_window = chosen < FLY
    select = ((target[None, :] == jnp.arange(FLY * CAP)[:, None]) & in_window[None, :]).astype(BF)
    select_tok = select.reshape(FLY * CAP, TOK, 2).sum(axis=2).astype(BF)
    hres, outbox = attention(
        queries[0], keys[0], values[0], resid[0], log_decay[0].T, attn_gain, moe_gain, select_tok
    )
    outbox = outbox.reshape(FLY, CAP, D)
    my_expert = lax.axis_index("ctx") // SHARDS
    mine = lax.dynamic_index_in_dim(
        lax.all_gather(outbox[None], "ctx", axis=0, tiled=True), my_expert, 1, False
    )
    count = mine.shape[0]
    hidden = jax.nn.gelu(dot(mine.reshape(count * CAP, D), w_up[0]), approximate=True).astype(BF)
    partial_value = dot(hidden, w_down[0]).astype(BF).reshape(count, CAP, D)
    returned = lax.all_to_all(partial_value, "ctx", split_axis=0, concat_axis=0, tiled=True)
    summed = returned.reshape(FLY, SHARDS, CAP, D).astype(F32).sum(axis=1)
    summed = summed.reshape(FLY * CAP, D)
    weighted = (select.astype(F32) * combine_weight[0].reshape(1, -1)).reshape(FLY * CAP, TOK, 2).sum(axis=2)
    mixed = lax.dot_general(weighted, summed, (((0,), (0,)), ((), ())), precision=HIGH, preferred_element_type=F32)
    layer_out = (hres + mixed).astype(BF)
    pairs = [(source, (source + 1) % 4) for source in range(4)]
    return lax.ppermute(layer_out[None], "section", pairs)


def solution(mesh):
    token = P("section", "ctx", None)
    return jax.shard_map(
        local,
        mesh=mesh,
        in_specs=(
            token, token, token, token, token,
            P("section", None), P("section", None),
            token, token,
            P("section", None, "ctx"), token,
        ),
        out_specs=token,
        check_vma=False,
    )
```

time: 711 us -> 355 us (0.50)
  the two profiles are of different devices: /device:TPU:0 before, /device:TPU:32 now
where the time goes in v1:
time: 355 us
  waiting for transfers between devices  215 us (61%)
  Pallas kernels  89 us (25%)
  matrix products  18.5 us (5%)
  between operations  13.5 us (4%)
  starting transfers between devices  8.03 us (2%)
  local copies, waits for them, and re-layouts  5.62 us (2%)
  other arithmetic  5.58 us (2%)
    all_gather x1, waiting for transfers between devices, local(): lax.all_gather(outbox[None], 'ctx', axis=0, tiled=True)  90.9 us
    pallas_call x1, Pallas kernels, attention(): pl.pallas_call(attention_kernel, out_shape=(jax.ShapeDtypeStruct((TOK, D)...  89 us
    all_to_all x1, waiting for transfers between devices, local(): lax.all_to_all(partial_value, 'ctx', split_axis=0, concat_axis=0, tiled=T...  88.2 us
    ppermute x1, waiting for transfers between devices, local(): return lax.ppermute(layer_out[None], 'section', pairs)  35.7 us
    dot_general x3, matrix products, dot(): return jnp.dot(a, b, preferred_element_type=F32)  15.7 us
  transfers between devices with their start and end apart: 3, of which 3 were waited for; matrix products, arithmetic and copies ran while one was open for 0% of the time, Pallas kernels for 0%

profile of v1, /device:TPU:32, one launch (start us, length us, event | category | flops | bytes accessed | tf_op | source)
XLA Modules:
  0.0 355.1 jit_solution(8257892773641424316)
XLA Ops:
  6.5 0.0 all-gather.2.cloned.1.call-start
  6.5 0.8 copy.23
  7.3 0.7 compare_bitcast_fusion
  8.0 0.1 eq.30
  8.1 0.2 fusion.17
  8.4 0.1 convert_element_type.46
  8.5 0.1 copy.25
  8.6 0.6 fusion.20.select_ref
  9.2 89.0 %attention.1 = (f32[128,6144]{1,0:T(8,128)}, bf16[64,6144]{1,0:T(8,128)(2,1)}) custom-call(bf16[128,6144]{1,0:T(8,128)(2,1)} %bitcast.38, bf16[128,6144]{1,0:T(8,128)(2,1)} %bitcast.39, bf16[128,6144]{1,0:T(8,128)(2,1)} %bitcast.40, bf16[128,6144]{1,0:T(8,128)(2,1)} %bitcast.41, f32[48,128]{1,0:T(8,128)} %bitcast.43, f32[1,6144]{1,0:T(1,128)} %attn_gain_ref.1, ...), custom_call_target="tpu_custom_call" | custom-call | tf_op jit(solution)/shard_map/attention/pallas_call | solution.py:314
  98.2 0.0 all-gather.2.cloned.1.call-update
  98.3 90.9 %all-gather.2.cloned.1.call-done = bf16[32,4,16,6144]{3,2,1,0:T(8,128)(2,1)} async-done(((bf16[1,4,16,6144]{3,2,1,0:T(8,128)(2,1)}), bf16[32,4,16,6144]{3,2,1,0:T(8,128)(2,1)}) %all-gather.2.cloned.1.call-update) | async-done | bytes 25165840 | tf_op jit(solution)/shard_map/all_gather | solution.py:376
  189.2 0.0 slice-start
  189.2 3.3 constant_dynamic-slice_fusion
  192.6 0.0 slice-start.1
  192.6 8.5 %fusion.14 = bf16[512,640]{1,0:T(8,128)(2,1)S(1)} fusion(bf16[512,6144]{1,0:T(8,128)(2,1)S(1)} %bitcast.36, bf16[1,6144,640]{2,1,0:T(8,128)(2,1)} %param.20), kind=kOutput, calls=%fused_computation.16 | convolution fusion | flops 4029480960 | bytes 14811136 | tf_op jit(solution)/shard_map/dot_general | solution.py:25
  201.1 0.0 slice-done
  201.1 0.0 slice-done.1
  201.1 6.9 %convolution_convert_fusion = bf16[512,6144]{1,0:T(8,128)(2,1)} fusion(bf16[512,640]{1,0:T(8,128)(2,1)S(1)} %fusion.14, bf16[1,640,6144]{2,1,0:T(8,128)(2,1)S(1)} %bitcast.46), kind=kOutput, calls=%fused_computation.1 | convolution fusion | flops 4029677568 | bytes 14811136 | tf_op jit(solution)/shard_map/dot_general | solution.py:25
  208.1 0.0 copy-start.1
  208.1 6.5 %all-to-all-start = ((bf16[32,16,6144]{2,1,0:T(8,128)(2,1)}), bf16[32,16,6144]{2,1,0:T(8,128)(2,1)}, u32[]{:S(2)}, u32[]{:S(2)}) async-start(bf16[32,16,6144]{2,1,0:T(8,128)(2,1)} %bitcast.35), calls=%async_computation | async-start | bytes 12582912 | tf_op jit(solution)/shard_map/all_to_all | solution.py:381
  214.6 0.0 copy-done.1
  214.6 88.2 %all-to-all-done = bf16[32,16,6144]{2,1,0:T(8,128)(2,1)} async-done(((bf16[32,16,6144]{2,1,0:T(8,128)(2,1)}), bf16[32,16,6144]{2,1,0:T(8,128)(2,1)}, u32[]{:S(2)}, u32[]{:S(2)}) %all-to-all-start) | async-done | bytes 6291488 | tf_op jit(solution)/shard_map/all_to_all | solution.py:381
  302.8 0.0 copy-start
  302.8 4.2 %convert_reduce_fusion = f32[4,16,6144]{2,1,0:T(8,128)S(1)} fusion(bf16[32,16,6144]{2,1,0:T(8,128)(2,1)} %all-to-all-done), kind=kLoop, calls=%fused_computation | loop fusion | flops 5898240 | bytes 7864320 | tf_op jit(solution)/shard_map/reduce_sum | solution.py:382
  307.0 0.0 copy-done
  307.0 2.9 fusion.4
  309.9 1.5 collective-permute-start
  311.4 35.7 %collective-permute-done = bf16[1,128,6144]{2,1,0:T(8,128)(2,1)S(1)} collective-permute-done((bf16[1,128,6144]{2,1,0:T(8,128)(2,1)S(1)}, bf16[1,128,6144]{2,1,0:T(8,128)(2,1)S(1)}, u32[]{:S(2)}, u32[]{:S(2)}) %collective-permute-start) | collective-permute-done | bytes 1572896 | tf_op jit(solution)/shard_map/ppermute | solution.py:388
  347.1 1.1 copy.27
  (4 shorter events, 0.0 us)
Async XLA Ops:
  6.5 182.7 %all-gather.2.cloned.1.call-start = ((), (), s32[]{:S(2)}) async-start(), calls=%async_computation.1 | async-start | bytes 25952256 | tf_op jit(solution)/shard_map/all_gather | solution.py:376
  189.2 11.9 %slice-start = ((s8[7864320]{0:T(1024)(128)(4,1)}), s8[4194304]{0:T(1024)(128)(4,1)S(1)}, s32[]{:S(2)}) async-start(s8[7864320]{0:T(1024)(128)(4,1)} %bitcast.45), calls=%async_computation.2 | async-start | bytes 8388608
  192.6 8.6 %slice-start.1 = ((s8[7864320]{0:T(1024)(128)(4,1)}), s8[3670016]{0:T(1024)(128)(4,1)S(1)}, s32[]{:S(2)}) async-start(s8[7864320]{0:T(1024)(128)(4,1)} %bitcast.45), calls=%async_computation.3 | async-start | bytes 7340032
  208.1 6.5 %copy-start.1 = (f32[1,128,2]{1,2,0:T(2,128)S(1)}, f32[1,128,2]{1,2,0:T(2,128)}, u32[]{:S(2)}) copy-start(f32[1,128,2]{1,2,0:T(2,128)} %param.19) | copy-start | bytes 3076
  208.1 94.7 %all-to-all-start = ((bf16[32,16,6144]{2,1,0:T(8,128)(2,1)}), bf16[32,16,6144]{2,1,0:T(8,128)(2,1)}, u32[]{:S(2)}, u32[]{:S(2)}) async-start(bf16[32,16,6144]{2,1,0:T(8,128)(2,1)} %bitcast.35), calls=%async_computation | async-start | bytes 12582912 | tf_op jit(solution)/shard_map/all_to_all | solution.py:381
  302.8 4.2 %copy-start = (f32[128,6144]{1,0:T(8,128)S(1)}, f32[128,6144]{1,0:T(8,128)}, u32[]{:S(2)}) copy-start(f32[128,6144]{1,0:T(8,128)} %get-tuple-element.7) | copy-start | bytes 9437188
  309.9 37.2 %collective-permute-start = (bf16[1,128,6144]{2,1,0:T(8,128)(2,1)S(1)}, bf16[1,128,6144]{2,1,0:T(8,128)(2,1)S(1)}, u32[]{:S(2)}, u32[]{:S(2)}) collective-permute-start(bf16[1,128,6144]{2,1,0:T(8,128)(2,1)S(1)} %fusion.4), channel_id=1, source_target_pairs={{0,32},{32,64},{64,96},{96,0},{1,33},{33,65},{65,97},{97,1},{2,34}... | collective-permute-start | bytes 4718600 | tf_op jit(solution)/shard_map/ppermute | solution.py:388
Sparse Core Ops, SparseCore 0:
  98.4 90.7 all-gather.1

commit v2 on v1

--- a/solution.py
+++ b/solution.py
@@ -49,7 +49,7 @@
 
 def attention_kernel(
     q_hbm, k_hbm, v_hbm, resid_hbm, rate_ref, attn_gain_ref, moe_gain_ref, select_ref,
-    hres_ref, outbox_ref,
+    high_ref, low_ref, outbox_ref,
     q_ref, k_ref, v_ref, resid_ref, cum_ref, total_ref, partner_total, own_state,
     partner_state, t_send, t_recv, within, r_send, r_recv, p_send, chip_prefix,
     f_send, prefix, attn_ref, square_ref,
@@ -287,7 +287,7 @@
 
     def residual(h, carry):
         out = resid_ref[:, columns(h)].astype(F32) + attn_ref[:, columns(h)] * scale * attn_gain_ref[:, columns(h)]
-        hres_ref[:, columns(h)] = out
+        attn_ref[:, columns(h)] = out
         square_ref[...] += out * out
         return carry
 
@@ -297,7 +297,11 @@
     select = select_ref[...]
 
     def norm(h, carry):
-        normed = (hres_ref[:, columns(h)] * scale_2 * moe_gain_ref[:, columns(h)]).astype(BF)
+        out = attn_ref[:, columns(h)]
+        high, low = parts(out)
+        high_ref[:, columns(h)] = high
+        low_ref[:, columns(h)] = dot(select, low).astype(BF)
+        normed = (out * scale_2 * moe_gain_ref[:, columns(h)]).astype(BF)
         outbox_ref[:, columns(h)] = dot(select, normed).astype(BF)
         return carry
 
@@ -314,11 +318,12 @@
     return pl.pallas_call(
         attention_kernel,
         out_shape=(
-            jax.ShapeDtypeStruct((TOK, D), F32),
+            jax.ShapeDtypeStruct((TOK, D), BF),
+            jax.ShapeDtypeStruct((FLY * CAP, D), BF),
             jax.ShapeDtypeStruct((FLY * CAP, D), BF),
         ),
         in_specs=[hbm] * 4 + [vmem] * 4,
-        out_specs=(vmem, vmem),
+        out_specs=(vmem, vmem, vmem),
         scratch_shapes=[
             pltpu.VMEM((TOK, D), BF),
             pltpu.VMEM((TOK, D), BF),
@@ -350,6 +355,266 @@
     )(queries, keys, values, resid, rate, attn_gain, moe_gain, select)
 
 
+BLOCK = 4 * CAP
+HALF = 2 * CAP
+STEP = 512
+UNITS = 640
+
+
+def window_kernel(
+    outbox_ref, high_ref, low_ref, mixing_ref, up_hbm, down_hbm,
+    out_ref,
+    up_ref, down_ref, rows_ref, part_ref, partner_part, total_ref, relay_in, relay_out,
+    near_in, far_in, final_ref, sums_ref, high_in, low_in, mixing_in,
+    load_sems, y_send, y_recv, core_send, core_recv, z_send, z_recv, hop_send, hop_recv,
+    part_send, part_recv, ring_send, ring_recv, next_send, next_recv,
+):
+    y, z, c = place()
+    section = lax.axis_index("section")
+    after = lax.rem(section + 1, 4)
+    before = lax.rem(section + 3, 4)
+    loads = [
+        pltpu.make_async_copy(up_hbm, up_ref, load_sems.at[0]),
+        pltpu.make_async_copy(down_hbm, down_ref, load_sems.at[1]),
+    ]
+    for load in loads:
+        load.start()
+    z_plus, z_minus, z_far = lax.rem(z + 1, 4), lax.rem(z + 3, 4), lax.rem(z + 2, 4)
+    partner = index_of(y, z, 1 - c)
+    plus, minus = index_of(y, z_plus, c), index_of(y, z_minus, c)
+    y_peer = [index_of(lax.rem(y + d, 4), z, c) for d in range(4)]
+    barrier = pltpu.get_barrier_semaphore()
+    for peer in [partner, plus, minus] + y_peer[1:]:
+        pl.semaphore_signal(barrier, inc=1, device_id={"ctx": peer})
+    for other in (after, before):
+        for peer in y_peer:
+            pl.semaphore_signal(barrier, inc=1, device_id={"section": other, "ctx": peer})
+    pl.semaphore_wait(barrier, 14)
+
+    sent = []
+
+    def send(src, dst, send_sem, recv_sem, peer, section_to=None):
+        target = {"ctx": peer} if section_to is None else {"section": section_to, "ctx": peer}
+        copy = pltpu.make_async_remote_copy(
+            src_ref=src, dst_ref=dst, send_sem=send_sem, recv_sem=recv_sem, device_id=target
+        )
+        copy.start()
+        sent.append(copy)
+
+    def arrived(dst, recv_sem, peer, section_to=None):
+        target = {"ctx": peer} if section_to is None else {"section": section_to, "ctx": peer}
+        pltpu.make_async_remote_copy(
+            src_ref=dst, dst_ref=dst, send_sem=recv_sem, recv_sem=recv_sem, device_id=target
+        ).wait_recv()
+
+    spot = (0, 2, 1, 3)
+
+    def piece(block, core, p):
+        return rows_ref.at[block, pl.ds(pl.multiple_of(core * BLOCK + p * CAP, CAP), CAP), :]
+
+    def box(e):
+        return outbox_ref.at[pl.ds(pl.multiple_of(e * CAP, CAP), CAP), :]
+
+    for d in (2, 1, 3):
+        send(
+            box(lax.rem(y + d, 4)), piece(z, c, spot[d]), y_send.at[d - 1], y_recv.at[d - 1], y_peer[d]
+        )
+    rows_ref[z, pl.ds(pl.multiple_of(c * BLOCK, CAP), CAP), :] = outbox_ref[
+        pl.ds(pl.multiple_of(y * CAP, CAP), CAP), :
+    ]
+
+    def spread(p):
+        src = piece(z, c, p)
+        send(src, src, z_send.at[0, p], z_recv.at[0, p], plus)
+        send(src, src, z_send.at[1, p], z_recv.at[1, p], minus)
+        send(src, src, core_send.at[0, p], core_recv.at[0, p], partner)
+
+    def from_minus(p):
+        src = piece(z_minus, c, p)
+        arrived(src, z_recv.at[0, p], minus)
+        if p < 2:
+            send(src, src, hop_send.at[p], hop_recv.at[p], plus)
+        send(src, src, core_send.at[1, p], core_recv.at[1, p], partner)
+
+    def from_plus(p):
+        src = piece(z_plus, c, p)
+        arrived(src, z_recv.at[1, p], plus)
+        if p >= 2:
+            send(src, src, hop_send.at[p], hop_recv.at[p], minus)
+        send(src, src, core_send.at[2, p], core_recv.at[2, p], partner)
+
+    def from_far(p):
+        src = piece(z_far, c, p)
+        arrived(src, hop_recv.at[p], minus if p < 2 else plus)
+        send(src, src, core_send.at[3, p], core_recv.at[3, p], partner)
+
+    spread(0)
+    send(high_ref, high_in, next_send.at[0], next_recv.at[0], y_peer[0], after)
+    send(low_ref, low_in, next_send.at[1], next_recv.at[1], y_peer[0], after)
+    send(mixing_ref, mixing_in, next_send.at[2], next_recv.at[2], y_peer[0], after)
+    for d in (1, 3, 2):
+        arrived(piece(z, c, spot[d]), y_recv.at[d - 1], y_peer[4 - d])
+        spread(spot[d])
+
+    blocks = (z, z_minus, z_plus, z_far)
+    for load in loads:
+        load.wait()
+
+    def compute(k):
+        block = blocks[k]
+        for p in range(4):
+            arrived(piece(block, 1 - c, p), core_recv.at[k, p], partner)
+        total_ref[...] = jnp.zeros_like(total_ref)
+
+        def up(i, carry):
+            at = pl.ds(pl.multiple_of(i * STEP, STEP), STEP)
+            total_ref[...] += dot(rows_ref[block, :, at], up_ref[at, :])
+            return carry
+
+        lax.fori_loop(0, D // STEP, up, 0)
+        hidden = jax.nn.gelu(total_ref[...], approximate=True).astype(BF)
+
+        def down(i, carry):
+            at = pl.ds(pl.multiple_of(i * STEP, STEP), STEP)
+            part_ref[block, :, at] = dot(hidden, down_ref[:, at]).astype(BF)
+            return carry
+
+        lax.fori_loop(0, D // STEP, down, 0)
+        other = part_ref.at[block, pl.ds(pl.multiple_of((1 - c) * BLOCK, BLOCK), BLOCK), :]
+        send(other, partner_part.at[k], part_send.at[k], part_recv.at[k], partner)
+
+    def own(k, half=None):
+        if half is None:
+            return part_ref.at[blocks[k], pl.ds(pl.multiple_of(c * BLOCK, BLOCK), BLOCK), :]
+        return part_ref.at[blocks[k], pl.ds(pl.multiple_of(c * BLOCK + half * HALF, HALF), HALF), :]
+
+    def over_columns(body):
+        def one(i, carry):
+            body(pl.ds(pl.multiple_of(i * STEP, STEP), STEP))
+            return carry
+
+        lax.fori_loop(0, D // STEP, one, 0)
+
+    def core_sum(k):
+        arrived(partner_part.at[k], part_recv.at[k], partner)
+        mine = own(k)
+
+        def add(at):
+            mine[:, at] = (mine[:, at].astype(F32) + partner_part[k, :, at].astype(F32)).astype(BF)
+
+        over_columns(add)
+
+    compute(0)
+    for p in (0, 1, 2, 3):
+        from_minus(p)
+        from_plus(p)
+    compute(1)
+    compute(2)
+    for p in (0, 2, 1, 3):
+        from_far(p)
+    core_sum(1)
+    send(own(1, 0), near_in.at[1], ring_send.at[1], ring_recv.at[1], minus)
+    core_sum(2)
+    send(own(2, 1), near_in.at[0], ring_send.at[0], ring_recv.at[0], plus)
+    compute(3)
+    core_sum(0)
+    core_sum(3)
+    send(own(3, 0), relay_in.at[0], ring_send.at[2], ring_recv.at[2], plus)
+    send(own(3, 1), relay_in.at[1], ring_send.at[3], ring_recv.at[3], minus)
+
+    def relay(side):
+        peer = (minus, plus)[side]
+        arrived(relay_in.at[side], ring_recv.at[2 + side], peer)
+        mine = own(2 - side, side)
+
+        def add(at):
+            relay_out[side, :, at] = (
+                mine[:, at].astype(F32) + relay_in[side, :, at].astype(F32)
+            ).astype(BF)
+
+        over_columns(add)
+        send(
+            relay_out.at[side], far_in.at[side], ring_send.at[4 + side], ring_recv.at[4 + side],
+            (plus, minus)[side],
+        )
+
+    relay(0)
+    relay(1)
+    arrived(near_in.at[0], ring_recv.at[0], minus)
+    arrived(near_in.at[1], ring_recv.at[1], plus)
+    arrived(far_in.at[0], ring_recv.at[4], minus)
+    arrived(far_in.at[1], ring_recv.at[5], plus)
+    for half in range(2):
+        mine = own(0, half)
+
+        def add(at, half=half, mine=mine):
+            final_ref[half * HALF : (half + 1) * HALF, at] = (
+                mine[:, at].astype(F32)
+                + near_in[1 - half, :, at].astype(F32)
+                + far_in[half, :, at].astype(F32)
+            ).astype(BF)
+
+        over_columns(add)
+        for d in ((0, 2), (1, 3))[half]:
+            p = spot[d]
+            send(
+                final_ref.at[p * CAP : (p + 1) * CAP, :],
+                sums_ref.at[pl.ds(pl.multiple_of(y * CAP, CAP), CAP), :],
+                next_send.at[3 + d], next_recv.at[3 + d], y_peer[(4 - d) % 4], after,
+            )
+    arrived(high_in, next_recv.at[0], y_peer[0], before)
+    arrived(low_in, next_recv.at[1], y_peer[0], before)
+    arrived(mixing_in, next_recv.at[2], y_peer[0], before)
+    for d in range(4):
+        arrived(sums_ref.at[0:CAP, :], next_recv.at[3 + d], y_peer[d], before)
+    first = mixing_in[:, :BLOCK].astype(BF)
+    weight_high, weight_low = parts(mixing_in[:, BLOCK:])
+
+    def mix(at):
+        sums = sums_ref[:, at]
+        mixed = dot(weight_high, sums) + dot(weight_low, sums)
+        out_ref[:, at] = ((high_in[:, at].astype(F32) + dot(first, low_in[:, at])) + mixed).astype(BF)
+
+    over_columns(mix)
+    for copy in sent:
+        copy.wait_send()
+
+
+def window(outbox, high, low, mixing, w_up, w_down):
+    vmem = pl.BlockSpec(memory_space=pltpu.VMEM)
+    hbm = pl.BlockSpec(memory_space=pl.ANY)
+    dma = pltpu.SemaphoreType.DMA
+    return pl.pallas_call(
+        window_kernel,
+        out_shape=jax.ShapeDtypeStruct((TOK, D), BF),
+        in_specs=[vmem] * 4 + [hbm] * 2,
+        out_specs=vmem,
+        scratch_shapes=[
+            pltpu.VMEM((D, UNITS), BF),
+            pltpu.VMEM((UNITS, D), BF),
+            pltpu.VMEM((4, 2 * BLOCK, D), BF),
+            pltpu.VMEM((4, 2 * BLOCK, D), BF),
+            pltpu.VMEM((4, BLOCK, D), BF),
+            pltpu.VMEM((2 * BLOCK, UNITS), F32),
+            pltpu.VMEM((2, HALF, D), BF),
+            pltpu.VMEM((2, HALF, D), BF),
+            pltpu.VMEM((2, HALF, D), BF),
+            pltpu.VMEM((2, HALF, D), BF),
+            pltpu.VMEM((BLOCK, D), BF),
+            pltpu.VMEM((BLOCK, D), BF),
+            pltpu.VMEM((TOK, D), BF),
+            pltpu.VMEM((BLOCK, D), BF),
+            pltpu.VMEM((TOK, 2 * BLOCK), F32),
+            dma((2,)), dma((3,)), dma((3,)), dma((4, 4)), dma((4, 4)), dma((2, 4)), dma((2, 4)),
+            dma((4,)), dma((4,)), dma((4,)), dma((4,)), dma((6,)), dma((6,)), dma((7,)), dma((7,)),
+        ],
+        compiler_params=pltpu.CompilerParams(
+            collective_id=1, has_side_effects=True, vmem_limit_bytes=60 * 2**20
+        ),
+        name="window",
+    )(outbox, high, low, mixing, w_up, w_down)
+
+
 def slots_of(chosen):
     count = chosen.shape[0]
     onehot = (chosen[:, None] == jnp.arange(EXPERTS)[None, :]).astype(BF)
@@ -367,25 +632,15 @@
     in_window = chosen < FLY
     select = ((target[None, :] == jnp.arange(FLY * CAP)[:, None]) & in_window[None, :]).astype(BF)
     select_tok = select.reshape(FLY * CAP, TOK, 2).sum(axis=2).astype(BF)
-    hres, outbox = attention(
+    high, low, outbox = attention(
         queries[0], keys[0], values[0], resid[0], log_decay[0].T, attn_gain, moe_gain, select_tok
     )
-    outbox = outbox.reshape(FLY, CAP, D)
-    my_expert = lax.axis_index("ctx") // SHARDS
-    mine = lax.dynamic_index_in_dim(
-        lax.all_gather(outbox[None], "ctx", axis=0, tiled=True), my_expert, 1, False
-    )
-    count = mine.shape[0]
-    hidden = jax.nn.gelu(dot(mine.reshape(count * CAP, D), w_up[0]), approximate=True).astype(BF)
-    partial_value = dot(hidden, w_down[0]).astype(BF).reshape(count, CAP, D)
-    returned = lax.all_to_all(partial_value, "ctx", split_axis=0, concat_axis=0, tiled=True)
-    summed = returned.reshape(FLY, SHARDS, CAP, D).astype(F32).sum(axis=1)
-    summed = summed.reshape(FLY * CAP, D)
-    weighted = (select.astype(F32) * combine_weight[0].reshape(1, -1)).reshape(FLY * CAP, TOK, 2).sum(axis=2)
-    mixed = lax.dot_general(weighted, summed, (((0,), (0,)), ((), ())), precision=HIGH, preferred_element_type=F32)
-    layer_out = (hres + mixed).astype(BF)
-    pairs = [(source, (source + 1) % 4) for source in range(4)]
-    return lax.ppermute(layer_out[None], "section", pairs)
+    pairs = select.T.reshape(TOK, 2, FLY * CAP).astype(F32)
+    inside = in_window.reshape(TOK, 2)
+    first = jnp.where(inside[:, 0:1], pairs[:, 0], pairs[:, 1])
+    weighted = (pairs * combine_weight[0][:, :, None]).sum(axis=1)
+    mixing = jnp.concatenate([first, weighted], axis=1)
+    return window(outbox, high, low, mixing, w_up[0], w_down[0])[None]
 
 
 def solution(mesh):

time: 355 us -> 202 us (0.57)
  the two profiles are of different devices: /device:TPU:32 before, /device:TPU:0 now
where the time goes in v2:
time: 202 us; the launch traced here: 201 us
  Pallas kernels  194 us (96%)
  local copies, waits for them, and re-layouts  3.81 us (2%)
  other arithmetic  3.12 us (2%)
    pallas_call x1, Pallas kernels, window(): pl.pallas_call(window_kernel, out_shape=jax.ShapeDtypeStruct((TOK, D), BF...  104 us
    pallas_call x1, Pallas kernels, attention(): pl.pallas_call(attention_kernel, out_shape=(jax.ShapeDtypeStruct((TOK, D)...  90.5 us

profile of v2, /device:TPU:0, one launch (start us, length us, event | category | flops | bytes accessed | tf_op | source)
XLA Modules:
  0.0 201.4 jit_solution(11917066240741365430)
XLA Ops:
  0.0 0.7 compare_bitcast_fusion
  0.7 0.8 copy.18
  1.5 0.1 eq.37
  1.6 0.2 fusion
  1.8 0.1 convert_element_type.33
  2.0 0.1 copy.20
  2.1 0.6 fusion.7.select_ref
  2.7 0.8 multiply_reduce_fusion
  3.6 0.1 fusion.3
  3.7 0.1 fusion.4
  3.8 0.7 pad_maximum_fusion.mixing_ref
  4.5 90.5 %attention.1 = (bf16[128,6144]{1,0:T(8,128)(2,1)}, bf16[64,6144]{1,0:T(8,128)(2,1)}, bf16[64,6144]{1,0:T(8,128)(2,1)}) custom-call(bf16[128,6144]{1,0:T(8,128)(2,1)} %bitcast.28, bf16[128,6144]{1,0:T(8,128)(2,1)} %bitcast.29, bf16[128,6144]{1,0:T(8,128)(2,1)} %bitcast.30, bf16[128,6144]{1,0:T(8,128)(2,1)} %bitcast.31, f32[48,128]{1,0:T(8,128)} %bitcast.32, ...), custom_call_target="tpu_custom_call" | custom-call | tf_op jit(solution)/shard_map/attention/pallas_call | solution.py:318
  95.0 103.7 %window.1 = bf16[128,6144]{1,0:T(8,128)(2,1)} custom-call(bf16[64,6144]{1,0:T(8,128)(2,1)} %get-tuple-element.8.outbox_ref, bf16[128,6144]{1,0:T(8,128)(2,1)} %get-tuple-element.9.high_ref, bf16[64,6144]{1,0:T(8,128)(2,1)} %get-tuple-element.10.low_ref, f32[128,128]{1,0:T(8,128)} %pad_maximum_fusion.mixing_ref, bf16[6144,640]{1,0:T(8,128)(2,1)} %bitcast.25, ...), custom_call_target="tpu_custom_call" | custom-call | tf_op jit(solution)/shard_map/window/pallas_call | solution.py:587
  198.7 2.7 %copy.23 = bf16[1,128,6144]{2,1,0:T(8,128)(2,1)} copy(bf16[1,128,6144]{2,1,0:T(8,128)(2,1)} %bitcast.27) | data formatting | bytes 3145728
  (3 shorter events, 0.0 us)

commit v3 on v2

--- a/solution.py
+++ b/solution.py
@@ -112,7 +112,7 @@
             own_state[1 - c, j, pl.ds(pl.multiple_of(i * HEAD, HEAD), HEAD), :] = state_of(h)
             return carry
 
-        lax.fori_loop(0, GROUP, one, 0)
+        lax.fori_loop(0, GROUP, one, 0, unroll=6)
         copy = remote(
             own_state.at[1 - c, j], partner_state.at[j], ps_send_sems.at[d], ps_recv_sems.at[d], partner
         )
@@ -130,7 +130,7 @@
             own_state[c, j, pl.ds(pl.multiple_of(i * HEAD, HEAD), HEAD), :] = state_of(h)
             return carry
 
-        lax.fori_loop(0, GROUP, one, 0)
+        lax.fori_loop(0, GROUP, one, 0, unroll=6)
         ps_copies[d].wait_recv()
         target = t_recv.at[0] if d == 0 else t_send.at[d - 1]
 
@@ -145,7 +145,7 @@
             target[pl.ds(ROWS + i, 1), :] = mine + other
             return carry
 
-        lax.fori_loop(0, GROUP, join, 0)
+        lax.fori_loop(0, GROUP, join, 0, unroll=2)
         target[ROWS + GROUP :, :] = jnp.zeros((8 - GROUP, HEAD), F32)
         if d:
             copy = remote(
@@ -167,7 +167,7 @@
         attn_ref[:, columns(h)] = dot(high, values) + dot(low, values)
         return carry
 
-    lax.fori_loop(0, 18, intra, 0)
+    lax.fori_loop(0, 18, intra, 0, unroll=6)
 
     for d in (1, 3, 2):
         t_copies[d].wait_recv()
@@ -188,14 +188,14 @@
         )
         return carry
 
-    lax.fori_loop(0, GROUP, row_sum, 0)
+    lax.fori_loop(0, GROUP, row_sum, 0, unroll=2)
     r_send[ROWS + GROUP :, :] = jnp.zeros((8 - GROUP, HEAD), F32)
     r_copies = {}
     for d in (2, 1, 3):
         copy = remote(r_send, r_recv.at[d], r_send_sems.at[d - 1], r_recv_sems.at[d - 1], y_peer[d])
         copy.start()
         r_copies[d] = copy
-    lax.fori_loop(18, 34, intra, 0)
+    lax.fori_loop(18, 36, intra, 0, unroll=6)
     r_recv[0] = r_send[...]
     for d in (1, 3, 2):
         r_copies[d].wait_recv()
@@ -211,7 +211,7 @@
         within[0, rows, :] = state
         return carry
 
-    lax.fori_loop(0, GROUP, row_prefix, 0)
+    lax.fori_loop(0, GROUP, row_prefix, 0, unroll=2)
     p_copies = {}
     for d in order:
         to = lax.rem(z + d, 4)
@@ -228,14 +228,14 @@
             target[rows, :] = start * jnp.exp(gone) + jnp.where(to > 0, within[jnp.maximum(to, 1), rows, :], 0.0)
             return carry
 
-        lax.fori_loop(0, GROUP, chip, 0)
+        lax.fori_loop(0, GROUP, chip, 0, unroll=2)
         if d:
             copy = remote(
                 target, chip_prefix.at[d], p_send_sems.at[d - 1], p_recv_sems.at[d - 1], z_peer[d]
             )
             copy.start()
             p_copies[d] = copy
-    lax.fori_loop(34, 48, intra, 0)
+    lax.fori_loop(36, 48, intra, 0, unroll=6)
 
     f_copies = {}
     for d in (0, 1, 3, 2):
@@ -254,7 +254,7 @@
             f_send[j, rows, :] = jnp.where(zero_first, full, base)
             return carry
 
-        lax.fori_loop(0, GROUP, core, 0)
+        lax.fori_loop(0, GROUP, core, 0, unroll=2)
         copy = remote(f_send.at[j], prefix.at[c, j], f_send_sems.at[d], f_recv_sems.at[d], partner)
         copy.start()
         f_copies[d] = copy
@@ -273,7 +273,7 @@
             square_ref[...] += out * out
             return carry
 
-        lax.fori_loop(0, GROUP, one, 0)
+        lax.fori_loop(0, GROUP, one, 0, unroll=6)
 
     for d in (0, 1, 3, 2):
         inter(c, lax.rem(z - d + 4, 4))
@@ -291,7 +291,7 @@
         square_ref[...] += out * out
         return carry
 
-    lax.fori_loop(0, HEADS, residual, 0)
+    lax.fori_loop(0, HEADS, residual, 0, unroll=6)
     scale_2 = lax.rsqrt(jnp.sum(square_ref[...], axis=1, keepdims=True) * (1.0 / D) + 1e-6)
     scale_2 = jnp.broadcast_to(scale_2, (TOK, HEAD))
     select = select_ref[...]
@@ -305,7 +305,7 @@
         outbox_ref[:, columns(h)] = dot(select, normed).astype(BF)
         return carry
 
-    lax.fori_loop(0, HEADS, norm, 0)
+    lax.fori_loop(0, HEADS, norm, 0, unroll=6)
     for copies in (ps_copies, t_copies, r_copies, p_copies, f_copies):
         for copy in copies.values():
             copy.wait_send()
@@ -357,17 +357,20 @@
 
 BLOCK = 4 * CAP
 HALF = 2 * CAP
-STEP = 512
+STEP = 1024
 UNITS = 640
+CHUNKS = 4
+WIDE = D // CHUNKS
+NARROW = 512
 
 
 def window_kernel(
     outbox_ref, high_ref, low_ref, mixing_ref, up_hbm, down_hbm,
     out_ref,
-    up_ref, down_ref, rows_ref, part_ref, partner_part, total_ref, relay_in, relay_out,
-    near_in, far_in, final_ref, sums_ref, high_in, low_in, mixing_in,
+    up_ref, down_ref, rows_ref, total_ref, hidden_ref, part_ref, partner_part, sum_ref,
+    relay_in, relay_out, near_in, far_in, final_ref, sums_ref, high_in, low_in, mixing_in,
     load_sems, y_send, y_recv, core_send, core_recv, z_send, z_recv, hop_send, hop_recv,
-    part_send, part_recv, ring_send, ring_recv, next_send, next_recv,
+    part_send, part_recv, ring_send, ring_recv, next_send, next_recv, sums_send, sums_recv,
 ):
     y, z, c = place()
     section = lax.axis_index("section")
@@ -379,9 +382,8 @@
     ]
     for load in loads:
         load.start()
-    z_plus, z_minus, z_far = lax.rem(z + 1, 4), lax.rem(z + 3, 4), lax.rem(z + 2, 4)
     partner = index_of(y, z, 1 - c)
-    plus, minus = index_of(y, z_plus, c), index_of(y, z_minus, c)
+    plus, minus = index_of(y, lax.rem(z + 1, 4), c), index_of(y, lax.rem(z + 3, 4), c)
     y_peer = [index_of(lax.rem(y + d, 4), z, c) for d in range(4)]
     barrier = pltpu.get_barrier_semaphore()
     for peer in [partner, plus, minus] + y_peer[1:]:
@@ -410,41 +412,40 @@
     spot = (0, 2, 1, 3)
 
     def piece(block, core, p):
-        return rows_ref.at[block, pl.ds(pl.multiple_of(core * BLOCK + p * CAP, CAP), CAP), :]
+        return rows_ref.at[pl.ds(pl.multiple_of((2 * block + core) * BLOCK + p * CAP, CAP), CAP), :]
 
     def box(e):
-        return outbox_ref.at[pl.ds(pl.multiple_of(e * CAP, CAP), CAP), :]
+        return pl.ds(pl.multiple_of(e * CAP, CAP), CAP)
 
     for d in (2, 1, 3):
         send(
-            box(lax.rem(y + d, 4)), piece(z, c, spot[d]), y_send.at[d - 1], y_recv.at[d - 1], y_peer[d]
+            outbox_ref.at[box(lax.rem(y + d, 4)), :], piece(0, c, spot[d]),
+            y_send.at[d - 1], y_recv.at[d - 1], y_peer[d],
         )
-    rows_ref[z, pl.ds(pl.multiple_of(c * BLOCK, CAP), CAP), :] = outbox_ref[
-        pl.ds(pl.multiple_of(y * CAP, CAP), CAP), :
-    ]
+    rows_ref[pl.ds(pl.multiple_of(c * BLOCK, CAP), CAP), :] = outbox_ref[box(y), :]
 
     def spread(p):
-        src = piece(z, c, p)
-        send(src, src, z_send.at[0, p], z_recv.at[0, p], plus)
-        send(src, src, z_send.at[1, p], z_recv.at[1, p], minus)
+        src = piece(0, c, p)
+        send(src, piece(1, c, p), z_send.at[0, p], z_recv.at[0, p], plus)
+        send(src, piece(2, c, p), z_send.at[1, p], z_recv.at[1, p], minus)
         send(src, src, core_send.at[0, p], core_recv.at[0, p], partner)
 
     def from_minus(p):
-        src = piece(z_minus, c, p)
+        src = piece(1, c, p)
         arrived(src, z_recv.at[0, p], minus)
         if p < 2:
-            send(src, src, hop_send.at[p], hop_recv.at[p], plus)
+            send(src, piece(3, c, p), hop_send.at[p], hop_recv.at[p], plus)
         send(src, src, core_send.at[1, p], core_recv.at[1, p], partner)
 
     def from_plus(p):
-        src = piece(z_plus, c, p)
+        src = piece(2, c, p)
         arrived(src, z_recv.at[1, p], plus)
         if p >= 2:
-            send(src, src, hop_send.at[p], hop_recv.at[p], minus)
+            send(src, piece(3, c, p), hop_send.at[p], hop_recv.at[p], minus)
         send(src, src, core_send.at[2, p], core_recv.at[2, p], partner)
 
     def from_far(p):
-        src = piece(z_far, c, p)
+        src = piece(3, c, p)
         arrived(src, hop_recv.at[p], minus if p < 2 else plus)
         send(src, src, core_send.at[3, p], core_recv.at[3, p], partner)
 
@@ -453,129 +454,140 @@
     send(low_ref, low_in, next_send.at[1], next_recv.at[1], y_peer[0], after)
     send(mixing_ref, mixing_in, next_send.at[2], next_recv.at[2], y_peer[0], after)
     for d in (1, 3, 2):
-        arrived(piece(z, c, spot[d]), y_recv.at[d - 1], y_peer[4 - d])
+        arrived(piece(0, c, spot[d]), y_recv.at[d - 1], y_peer[4 - d])
         spread(spot[d])
-
-    blocks = (z, z_minus, z_plus, z_far)
-    for load in loads:
-        load.wait()
-
-    def compute(k):
-        block = blocks[k]
-        for p in range(4):
-            arrived(piece(block, 1 - c, p), core_recv.at[k, p], partner)
-        total_ref[...] = jnp.zeros_like(total_ref)
-
-        def up(i, carry):
+    for p in (0, 2, 3, 1):
+        from_minus(p)
+        from_plus(p)
+
+    def up(blocks):
+        first, count = blocks[0] * 2 * BLOCK, len(blocks) * 2 * BLOCK
+        for block in blocks:
+            for p in range(4):
+                arrived(piece(block, 1 - c, p), core_recv.at[block, p], partner)
+        total_ref[:count, :] = jnp.zeros((count, UNITS), F32)
+
+        def one(i, carry):
             at = pl.ds(pl.multiple_of(i * STEP, STEP), STEP)
-            total_ref[...] += dot(rows_ref[block, :, at], up_ref[at, :])
-            return carry
-
-        lax.fori_loop(0, D // STEP, up, 0)
-        hidden = jax.nn.gelu(total_ref[...], approximate=True).astype(BF)
-
-        def down(i, carry):
-            at = pl.ds(pl.multiple_of(i * STEP, STEP), STEP)
-            part_ref[block, :, at] = dot(hidden, down_ref[:, at]).astype(BF)
-            return carry
-
-        lax.fori_loop(0, D // STEP, down, 0)
-        other = part_ref.at[block, pl.ds(pl.multiple_of((1 - c) * BLOCK, BLOCK), BLOCK), :]
-        send(other, partner_part.at[k], part_send.at[k], part_recv.at[k], partner)
-
-    def own(k, half=None):
-        if half is None:
-            return part_ref.at[blocks[k], pl.ds(pl.multiple_of(c * BLOCK, BLOCK), BLOCK), :]
-        return part_ref.at[blocks[k], pl.ds(pl.multiple_of(c * BLOCK + half * HALF, HALF), HALF), :]
+            total_ref[:count, :] += dot(rows_ref[first : first + count, at], up_ref[at, :])
+            return carry
+
+        lax.fori_loop(0, D // STEP, one, 0)
+        hidden_ref[first : first + count, :] = jax.nn.gelu(
+            total_ref[:count, :], approximate=True
+        ).astype(BF)
+
+    loads[0].wait()
+    up((0, 1, 2))
+    for p in (0, 2, 3, 1):
+        from_far(p)
+    up((3,))
+    loads[1].wait()
+
+    def down(q):
+        for i in range(WIDE // NARROW):
+            at = slice(i * NARROW, (i + 1) * NARROW)
+            out = dot(hidden_ref[...], down_ref[:, q * WIDE + i * NARROW : q * WIDE + (i + 1) * NARROW])
+            out = out.astype(BF)
+            for block in range(4):
+                for core in range(2):
+                    row = (2 * block + core) * BLOCK
+                    part_ref[q, core, block * BLOCK : (block + 1) * BLOCK, at] = out[row : row + BLOCK, :]
+        send(part_ref.at[q, 1 - c], partner_part.at[q], part_send.at[q], part_recv.at[q], partner)
 
     def over_columns(body):
         def one(i, carry):
-            body(pl.ds(pl.multiple_of(i * STEP, STEP), STEP))
-            return carry
-
-        lax.fori_loop(0, D // STEP, one, 0)
-
-    def core_sum(k):
-        arrived(partner_part.at[k], part_recv.at[k], partner)
-        mine = own(k)
+            body(pl.ds(pl.multiple_of(i * NARROW, NARROW), NARROW))
+            return carry
+
+        lax.fori_loop(0, WIDE // NARROW, one, 0)
+
+    def share(q, block, half):
+        first = block * BLOCK + half * HALF
+        return sum_ref.at[q, first : first + HALF, :]
+
+    def core_sum(q):
+        arrived(partner_part.at[q], part_recv.at[q], partner)
 
         def add(at):
-            mine[:, at] = (mine[:, at].astype(F32) + partner_part[k, :, at].astype(F32)).astype(BF)
+            sum_ref[q, :, at] = (
+                part_ref[q, c, :, at].astype(F32) + partner_part[q, :, at].astype(F32)
+            ).astype(BF)
 
         over_columns(add)
-
-    compute(0)
-    for p in (0, 1, 2, 3):
-        from_minus(p)
-        from_plus(p)
-    compute(1)
-    compute(2)
-    for p in (0, 2, 1, 3):
-        from_far(p)
+        send(share(q, 3, 0), relay_in.at[q, 0], ring_send.at[q, 2], ring_recv.at[q, 2], plus)
+        send(share(q, 3, 1), relay_in.at[q, 1], ring_send.at[q, 3], ring_recv.at[q, 3], minus)
+        send(share(q, 2, 1), near_in.at[q, 0], ring_send.at[q, 0], ring_recv.at[q, 0], plus)
+        send(share(q, 1, 0), near_in.at[q, 1], ring_send.at[q, 1], ring_recv.at[q, 1], minus)
+
+    def relay(q):
+        for side in range(2):
+            arrived(relay_in.at[q, side], ring_recv.at[q, 2 + side], (minus, plus)[side])
+            mine = share(q, 2 - side, side)
+
+            def add(at, side=side, mine=mine):
+                relay_out[q, side, :, at] = (
+                    mine[:, at].astype(F32) + relay_in[q, side, :, at].astype(F32)
+                ).astype(BF)
+
+            over_columns(add)
+            send(
+                relay_out.at[q, side], far_in.at[q, side],
+                ring_send.at[q, 4 + side], ring_recv.at[q, 4 + side], (plus, minus)[side],
+            )
+
+    def final(q):
+        arrived(near_in.at[q, 0], ring_recv.at[q, 0], minus)
+        arrived(near_in.at[q, 1], ring_recv.at[q, 1], plus)
+        arrived(far_in.at[q, 0], ring_recv.at[q, 4], minus)
+        arrived(far_in.at[q, 1], ring_recv.at[q, 5], plus)
+        for half in range(2):
+            mine = share(q, 0, half)
+
+            def add(at, half=half, mine=mine):
+                final_ref[q, half * HALF : (half + 1) * HALF, at] = (
+                    mine[:, at].astype(F32)
+                    + near_in[q, 1 - half, :, at].astype(F32)
+                    + far_in[q, half, :, at].astype(F32)
+                ).astype(BF)
+
+            over_columns(add)
+            for d in ((0, 2), (1, 3))[half]:
+                p = spot[d]
+                send(
+                    final_ref.at[q, p * CAP : (p + 1) * CAP, :], sums_ref.at[q, box(y), :],
+                    sums_send.at[q, d], sums_recv.at[q, d], y_peer[(4 - d) % 4], after,
+                )
+
+    down(0)
+    down(1)
+    core_sum(0)
+    down(2)
     core_sum(1)
-    send(own(1, 0), near_in.at[1], ring_send.at[1], ring_recv.at[1], minus)
+    relay(0)
+    down(3)
     core_sum(2)
-    send(own(2, 1), near_in.at[0], ring_send.at[0], ring_recv.at[0], plus)
-    compute(3)
-    core_sum(0)
+    relay(1)
+    final(0)
     core_sum(3)
-    send(own(3, 0), relay_in.at[0], ring_send.at[2], ring_recv.at[2], plus)
-    send(own(3, 1), relay_in.at[1], ring_send.at[3], ring_recv.at[3], minus)
-
-    def relay(side):
-        peer = (minus, plus)[side]
-        arrived(relay_in.at[side], ring_recv.at[2 + side], peer)
-        mine = own(2 - side, side)
-
-        def add(at):
-            relay_out[side, :, at] = (
-                mine[:, at].astype(F32) + relay_in[side, :, at].astype(F32)
-            ).astype(BF)
-
-        over_columns(add)
-        send(
-            relay_out.at[side], far_in.at[side], ring_send.at[4 + side], ring_recv.at[4 + side],
-            (plus, minus)[side],
-        )
-
-    relay(0)
-    relay(1)
-    arrived(near_in.at[0], ring_recv.at[0], minus)
-    arrived(near_in.at[1], ring_recv.at[1], plus)
-    arrived(far_in.at[0], ring_recv.at[4], minus)
-    arrived(far_in.at[1], ring_recv.at[5], plus)
-    for half in range(2):
-        mine = own(0, half)
-
-        def add(at, half=half, mine=mine):
-            final_ref[half * HALF : (half + 1) * HALF, at] = (
-                mine[:, at].astype(F32)
-                + near_in[1 - half, :, at].astype(F32)
-                + far_in[half, :, at].astype(F32)
-            ).astype(BF)
-
-        over_columns(add)
-        for d in ((0, 2), (1, 3))[half]:
-            p = spot[d]
-            send(
-                final_ref.at[p * CAP : (p + 1) * CAP, :],
-                sums_ref.at[pl.ds(pl.multiple_of(y * CAP, CAP), CAP), :],
-                next_send.at[3 + d], next_recv.at[3 + d], y_peer[(4 - d) % 4], after,
-            )
+    relay(2)
+    final(1)
+    relay(3)
+    final(2)
+    final(3)
     arrived(high_in, next_recv.at[0], y_peer[0], before)
     arrived(low_in, next_recv.at[1], y_peer[0], before)
     arrived(mixing_in, next_recv.at[2], y_peer[0], before)
-    for d in range(4):
-        arrived(sums_ref.at[0:CAP, :], next_recv.at[3 + d], y_peer[d], before)
     first = mixing_in[:, :BLOCK].astype(BF)
     weight_high, weight_low = parts(mixing_in[:, BLOCK:])
-
-    def mix(at):
-        sums = sums_ref[:, at]
-        mixed = dot(weight_high, sums) + dot(weight_low, sums)
-        out_ref[:, at] = ((high_in[:, at].astype(F32) + dot(first, low_in[:, at])) + mixed).astype(BF)
-
-    over_columns(mix)
+    for q in range(CHUNKS):
+        for d in range(4):
+            arrived(sums_ref.at[q, 0:CAP, :], sums_recv.at[q, d], y_peer[d], before)
+        for i in range(WIDE // NARROW):
+            sums = sums_ref[q, :, i * NARROW : (i + 1) * NARROW]
+            at = slice(q * WIDE + i * NARROW, q * WIDE + (i + 1) * NARROW)
+            mixed = dot(weight_high, sums) + dot(weight_low, sums)
+            out_ref[:, at] = ((high_in[:, at].astype(F32) + dot(first, low_in[:, at])) + mixed).astype(BF)
     for copy in sent:
         copy.wait_send()
 
@@ -592,21 +604,24 @@
         scratch_shapes=[
             pltpu.VMEM((D, UNITS), BF),
             pltpu.VMEM((UNITS, D), BF),
-            pltpu.VMEM((4, 2 * BLOCK, D), BF),
-            pltpu.VMEM((4, 2 * BLOCK, D), BF),
-            pltpu.VMEM((4, BLOCK, D), BF),
-            pltpu.VMEM((2 * BLOCK, UNITS), F32),
-            pltpu.VMEM((2, HALF, D), BF),
-            pltpu.VMEM((2, HALF, D), BF),
-            pltpu.VMEM((2, HALF, D), BF),
-            pltpu.VMEM((2, HALF, D), BF),
-            pltpu.VMEM((BLOCK, D), BF),
-            pltpu.VMEM((BLOCK, D), BF),
+            pltpu.VMEM((8 * BLOCK, D), BF),
+            pltpu.VMEM((6 * BLOCK, UNITS), F32),
+            pltpu.VMEM((8 * BLOCK, UNITS), BF),
+            pltpu.VMEM((CHUNKS, 2, 4 * BLOCK, WIDE), BF),
+            pltpu.VMEM((CHUNKS, 4 * BLOCK, WIDE), BF),
+            pltpu.VMEM((CHUNKS, 4 * BLOCK, WIDE), BF),
+            pltpu.VMEM((CHUNKS, 2, HALF, WIDE), BF),
+            pltpu.VMEM((CHUNKS, 2, HALF, WIDE), BF),
+            pltpu.VMEM((CHUNKS, 2, HALF, WIDE), BF),
+            pltpu.VMEM((CHUNKS, 2, HALF, WIDE), BF),
+            pltpu.VMEM((CHUNKS, BLOCK, WIDE), BF),
+            pltpu.VMEM((CHUNKS, BLOCK, WIDE), BF),
             pltpu.VMEM((TOK, D), BF),
             pltpu.VMEM((BLOCK, D), BF),
             pltpu.VMEM((TOK, 2 * BLOCK), F32),
             dma((2,)), dma((3,)), dma((3,)), dma((4, 4)), dma((4, 4)), dma((2, 4)), dma((2, 4)),
-            dma((4,)), dma((4,)), dma((4,)), dma((4,)), dma((6,)), dma((6,)), dma((7,)), dma((7,)),
+            dma((4,)), dma((4,)), dma((CHUNKS,)), dma((CHUNKS,)), dma((CHUNKS, 6)), dma((CHUNKS, 6)),
+            dma((3,)), dma((3,)), dma((CHUNKS, 4)), dma((CHUNKS, 4)),
         ],
         compiler_params=pltpu.CompilerParams(
             collective_id=1, has_side_effects=True, vmem_limit_bytes=60 * 2**20

time: 202 us -> 169 us (0.84)
  Pallas kernels: 194 us -> 161 us
    pallas_call x1, Pallas kernels: 104 us -> 85.5 us  [window(): pl.pallas_call(window_kernel, out_shape=jax.ShapeDtypeStruct((TOK, D), BF...]
    pallas_call x1, Pallas kernels: 90.5 us -> 75.7 us  [attention(): pl.pallas_call(attention_kernel, out_shape=(jax.ShapeDtypeStruct((TOK, D)...]
where the time goes in v3:
time: 169 us; the launch traced here: 168 us
  Pallas kernels  161 us (95%)
  local copies, waits for them, and re-layouts  3.81 us (2%)
  other arithmetic  3.12 us (2%)
    pallas_call x1, Pallas kernels, window(): pl.pallas_call(window_kernel, out_shape=jax.ShapeDtypeStruct((TOK, D), BF...  85.5 us
    pallas_call x1, Pallas kernels, attention(): pl.pallas_call(attention_kernel, out_shape=(jax.ShapeDtypeStruct((TOK, D)...  75.7 us
    unnamed x2, local copies, waits for them, and re-layouts  3.47 us

profile of v3, /device:TPU:0, one launch (start us, length us, event | category | flops | bytes accessed | tf_op | source)
XLA Modules:
  0.0 168.4 jit_solution(7027434780111929349)
XLA Ops:
  0.0 0.7 compare_bitcast_fusion
  0.7 0.8 copy.18
  1.5 0.1 eq.37
  1.6 0.2 fusion
  1.8 0.1 convert_element_type.33
  2.0 0.1 copy.20
  2.1 0.6 fusion.7.select_ref
  2.7 0.8 multiply_reduce_fusion
  3.6 0.1 fusion.3
  3.7 0.1 fusion.4
  3.8 0.7 pad_maximum_fusion.mixing_ref
  4.5 75.7 %attention.1 = (bf16[128,6144]{1,0:T(8,128)(2,1)}, bf16[64,6144]{1,0:T(8,128)(2,1)}, bf16[64,6144]{1,0:T(8,128)(2,1)}) custom-call(bf16[128,6144]{1,0:T(8,128)(2,1)} %bitcast.28, bf16[128,6144]{1,0:T(8,128)(2,1)} %bitcast.29, bf16[128,6144]{1,0:T(8,128)(2,1)} %bitcast.30, bf16[128,6144]{1,0:T(8,128)(2,1)} %bitcast.31, f32[48,128]{1,0:T(8,128)} %bitcast.32, ...), custom_call_target="tpu_custom_call" | custom-call | tf_op jit(solution)/shard_map/attention/pallas_call | solution.py:318
  80.2 85.5 %window.1 = bf16[128,6144]{1,0:T(8,128)(2,1)} custom-call(bf16[64,6144]{1,0:T(8,128)(2,1)} %get-tuple-element.8.outbox_ref, bf16[128,6144]{1,0:T(8,128)(2,1)} %get-tuple-element.9.high_ref, bf16[64,6144]{1,0:T(8,128)(2,1)} %get-tuple-element.10.low_ref, f32[128,128]{1,0:T(8,128)} %pad_maximum_fusion.mixing_ref, bf16[6144,640]{1,0:T(8,128)(2,1)} %bitcast.25, ...), custom_call_target="tpu_custom_call" | custom-call | tf_op jit(solution)/shard_map/window/pallas_call | solution.py:599
  165.7 2.7 %copy.23 = bf16[1,128,6144]{2,1,0:T(8,128)(2,1)} copy(bf16[1,128,6144]{2,1,0:T(8,128)(2,1)} %bitcast.27) | data formatting | bytes 3145728
  (3 shorter events, 0.0 us)

commit v4 on v3

--- a/solution.py
+++ b/solution.py
@@ -13,8 +13,8 @@
 SHARDS = 8
 CAP = 16
 FLY = 4
-GROUP = 6
-ROWS = GROUP * HEAD
+SUB = 2
+ROWS = SUB * HEAD
 MESSAGE = ROWS + 8
 BF = jnp.bfloat16
 F32 = jnp.float32
@@ -81,19 +81,18 @@
     total_ref[...] = jnp.dot(
         rate, jnp.ones((TOK, TOK), F32), precision=HIGH, preferred_element_type=F32
     )
-    pl.semaphore_wait(barrier, 7)
-
-    def remote(src, dst, send, recv, peer):
+    copies = []
+
+    def remote(src, dst, send_sem, recv_sem, peer):
         copy = pltpu.make_async_remote_copy(
-            src_ref=src, dst_ref=dst, send_sem=send, recv_sem=recv, device_id={"ctx": peer}
+            src_ref=src, dst_ref=dst, send_sem=send_sem, recv_sem=recv_sem, device_id={"ctx": peer}
         )
+        copy.start()
+        copies.append(copy)
         return copy
 
-    started = []
-    totals = remote(total_ref, partner_total, small_sems.at[0], small_sems.at[1], partner)
-    totals.start()
-    loads[0].wait()
-    loads[1].wait()
+    def tile(i):
+        return pl.ds(pl.multiple_of(i * HEAD, HEAD), HEAD)
 
     def state_of(h):
         row = jnp.exp(total_ref[pl.ds(h, 1), :] - cum_ref[pl.ds(h, 1), :])
@@ -102,184 +101,183 @@
         values = v_ref[:, columns(h)]
         return dot(high, values) + dot(low, values)
 
+    def states(half, s):
+        def one(n, carry):
+            own_state[half, s, tile(n), :] = state_of(half * 24 + s * 8 + n)
+            return carry
+
+        lax.fori_loop(0, 8, one, 0, unroll=8)
+
+    loads[0].wait()
+    loads[1].wait()
+    states(1 - c, 0)
+    pl.semaphore_wait(barrier, 7)
+    totals = remote(total_ref, partner_total, small_sems.at[0], small_sems.at[1], partner)
+    zero_first = c == 0
+
+    def swap(s):
+        return remote(
+            own_state.at[1 - c, s], partner_state.at[s], ps_send_sems.at[s], ps_recv_sems.at[s], partner
+        )
+
     order = (2, 1, 3, 0)
-    ps_copies = {}
-    for d in order:
-        j = lax.rem(z + d, 4)
-
-        def one(i, carry, j=j):
-            h = (1 - c) * 24 + j * GROUP + i
-            own_state[1 - c, j, pl.ds(pl.multiple_of(i * HEAD, HEAD), HEAD), :] = state_of(h)
+    t_copies = {}
+
+    def join(s):
+        for d in order:
+            j = lax.rem(z + d, 4)
+            target = t_recv.at[s, 0] if d == 0 else t_send.at[s, d - 1]
+            for i in range(SUB):
+                h = c * 24 + s * 8 + j * SUB + i
+                rows = tile(j * SUB + i)
+                mine = total_ref[pl.ds(h, 1), :]
+                other = partner_total[pl.ds(h, 1), :]
+                keep = jnp.exp(jnp.where(zero_first, other, 0.0))
+                take = jnp.exp(jnp.where(zero_first, 0.0, mine))
+                target[i * HEAD : (i + 1) * HEAD, :] = (
+                    keep * own_state[c, s, rows, :] + take * partner_state[s, rows, :]
+                )
+                target[ROWS + i : ROWS + i + 1, :] = mine + other
+            target[ROWS + SUB :, :] = jnp.zeros((8 - SUB, HEAD), F32)
+            if d:
+                t_copies[s, d] = remote(
+                    target, t_recv.at[s, d], t_send_sems.at[s, d - 1], t_recv_sems.at[s, d - 1], z_peer[d]
+                )
+
+    lower = earlier >= later
+
+    def intra(first, last):
+        def one(h, carry):
+            across = jnp.broadcast_to(cum_ref[pl.ds(h, 1), :], (TOK, TOK))
+            weights = jnp.exp(jnp.where(lower, across.T - across, -1e30))
+            scores = dot_t(q_ref[:, columns(h)], k_ref[:, columns(h)]) * weights
+            high, low = parts(scores)
+            values = v_ref[:, columns(h)]
+            attn_ref[:, columns(h)] = dot(high, values) + dot(low, values)
             return carry
 
-        lax.fori_loop(0, GROUP, one, 0, unroll=6)
-        copy = remote(
-            own_state.at[1 - c, j], partner_state.at[j], ps_send_sems.at[d], ps_recv_sems.at[d], partner
-        )
-        copy.start()
-        ps_copies[d] = copy
-    totals.wait()
-
-    zero_first = c == 0
-    t_copies = {}
-    for d in order:
-        j = lax.rem(z + d, 4)
-
-        def one(i, carry, j=j):
-            h = c * 24 + j * GROUP + i
-            own_state[c, j, pl.ds(pl.multiple_of(i * HEAD, HEAD), HEAD), :] = state_of(h)
-            return carry
-
-        lax.fori_loop(0, GROUP, one, 0, unroll=6)
-        ps_copies[d].wait_recv()
-        target = t_recv.at[0] if d == 0 else t_send.at[d - 1]
-
-        def join(i, carry, j=j, target=target):
-            h = c * 24 + j * GROUP + i
-            mine = total_ref[pl.ds(h, 1), :]
-            other = partner_total[pl.ds(h, 1), :]
-            keep = jnp.exp(jnp.where(zero_first, other, 0.0))
-            take = jnp.exp(jnp.where(zero_first, 0.0, mine))
-            rows = pl.ds(pl.multiple_of(i * HEAD, HEAD), HEAD)
-            target[rows, :] = keep * own_state[c, j, rows, :] + take * partner_state[j, rows, :]
-            target[pl.ds(ROWS + i, 1), :] = mine + other
-            return carry
-
-        lax.fori_loop(0, GROUP, join, 0, unroll=2)
-        target[ROWS + GROUP :, :] = jnp.zeros((8 - GROUP, HEAD), F32)
-        if d:
-            copy = remote(
-                target, t_recv.at[d], t_send_sems.at[d - 1], t_recv_sems.at[d - 1], z_peer[d]
+        lax.fori_loop(first, last, one, 0, unroll=6)
+
+    r_copies = {}
+
+    def row_sum(s):
+        for d in (1, 3, 2):
+            t_copies[s, d].wait_recv()
+        for i in range(SUB):
+            rows = slice(i * HEAD, (i + 1) * HEAD)
+            label = slice(ROWS + i, ROWS + i + 1)
+            state = t_recv[s, z, rows, :]
+            within[s, 1, rows, :] = state
+            for other in range(1, 4):
+                slot = lax.rem(z - other + 4, 4)
+                state = state * jnp.exp(t_recv[s, slot, label, :]) + t_recv[s, slot, rows, :]
+                if other < 3:
+                    within[s, other + 1, rows, :] = state
+            r_send[s, rows, :] = state
+            r_send[s, label, :] = (
+                t_recv[s, 0, label, :] + t_recv[s, 1, label, :]
+                + t_recv[s, 2, label, :] + t_recv[s, 3, label, :]
             )
-            copy.start()
-            t_copies[d] = copy
-
-    loads[2].wait()
-    lower = earlier >= later
-
-    def intra(h, carry):
-        cum = cum_ref[pl.ds(h, 1), :]
-        across = jnp.broadcast_to(cum, (TOK, TOK))
-        weights = jnp.exp(jnp.where(lower, across.T - across, -1e30))
-        scores = dot_t(q_ref[:, columns(h)], k_ref[:, columns(h)]) * weights
-        high, low = parts(scores)
-        values = v_ref[:, columns(h)]
-        attn_ref[:, columns(h)] = dot(high, values) + dot(low, values)
-        return carry
-
-    lax.fori_loop(0, 18, intra, 0, unroll=6)
-
-    for d in (1, 3, 2):
-        t_copies[d].wait_recv()
-
-    def row_sum(i, carry):
-        rows = pl.ds(pl.multiple_of(i * HEAD, HEAD), HEAD)
-        label = pl.ds(ROWS + i, 1)
-        state = t_recv[z, rows, :]
-        within[1, rows, :] = state
-        for other in range(1, 4):
-            slot = lax.rem(z - other + 4, 4)
-            state = state * jnp.exp(t_recv[slot, label, :]) + t_recv[slot, rows, :]
-            if other < 3:
-                within[other + 1, rows, :] = state
-        r_send[rows, :] = state
-        r_send[label, :] = (
-            t_recv[0, label, :] + t_recv[1, label, :] + t_recv[2, label, :] + t_recv[3, label, :]
-        )
-        return carry
-
-    lax.fori_loop(0, GROUP, row_sum, 0, unroll=2)
-    r_send[ROWS + GROUP :, :] = jnp.zeros((8 - GROUP, HEAD), F32)
-    r_copies = {}
-    for d in (2, 1, 3):
-        copy = remote(r_send, r_recv.at[d], r_send_sems.at[d - 1], r_recv_sems.at[d - 1], y_peer[d])
-        copy.start()
-        r_copies[d] = copy
-    lax.fori_loop(18, 36, intra, 0, unroll=6)
-    r_recv[0] = r_send[...]
-    for d in (1, 3, 2):
-        r_copies[d].wait_recv()
-
-    def row_prefix(i, carry):
-        rows = pl.ds(pl.multiple_of(i * HEAD, HEAD), HEAD)
-        label = pl.ds(ROWS + i, 1)
-        state = jnp.zeros((HEAD, HEAD), F32)
-        for other in range(3):
-            slot = lax.rem(y - other + 4, 4)
-            joined = state * jnp.exp(r_recv[slot, label, :]) + r_recv[slot, rows, :]
-            state = jnp.where(other < y, joined, state)
-        within[0, rows, :] = state
-        return carry
-
-    lax.fori_loop(0, GROUP, row_prefix, 0, unroll=2)
+        r_send[s, ROWS + SUB :, :] = jnp.zeros((8 - SUB, HEAD), F32)
+        for d in (2, 1, 3):
+            r_copies[s, d] = remote(
+                r_send.at[s], r_recv.at[s, d], r_send_sems.at[s, d - 1], r_recv_sems.at[s, d - 1], y_peer[d]
+            )
+        r_recv[s, 0] = r_send[s]
+
     p_copies = {}
-    for d in order:
-        to = lax.rem(z + d, 4)
-        target = chip_prefix.at[0] if d == 0 else p_send.at[d - 1]
-
-        def chip(i, carry, to=to, target=target):
-            rows = pl.ds(pl.multiple_of(i * HEAD, HEAD), HEAD)
-            label = pl.ds(ROWS + i, 1)
-            gone = jnp.zeros((1, HEAD), F32)
+
+    def chip_prefixes(s):
+        for d in (1, 3, 2):
+            r_copies[s, d].wait_recv()
+        for i in range(SUB):
+            rows = slice(i * HEAD, (i + 1) * HEAD)
+            label = slice(ROWS + i, ROWS + i + 1)
+            state = jnp.zeros((HEAD, HEAD), F32)
             for other in range(3):
-                slot = lax.rem(z - other + 4, 4)
-                gone = gone + jnp.where(other < to, t_recv[slot, label, :], 0.0)
-            start = within[0, rows, :]
-            target[rows, :] = start * jnp.exp(gone) + jnp.where(to > 0, within[jnp.maximum(to, 1), rows, :], 0.0)
-            return carry
-
-        lax.fori_loop(0, GROUP, chip, 0, unroll=2)
-        if d:
-            copy = remote(
-                target, chip_prefix.at[d], p_send_sems.at[d - 1], p_recv_sems.at[d - 1], z_peer[d]
-            )
-            copy.start()
-            p_copies[d] = copy
-    lax.fori_loop(36, 48, intra, 0, unroll=6)
+                slot = lax.rem(y - other + 4, 4)
+                joined = state * jnp.exp(r_recv[s, slot, label, :]) + r_recv[s, slot, rows, :]
+                state = jnp.where(other < y, joined, state)
+            within[s, 0, rows, :] = state
+        for d in order:
+            to = lax.rem(z + d, 4)
+            target = chip_prefix.at[s, 0] if d == 0 else p_send.at[s, d - 1]
+            for i in range(SUB):
+                rows = slice(i * HEAD, (i + 1) * HEAD)
+                label = slice(ROWS + i, ROWS + i + 1)
+                gone = jnp.zeros((1, HEAD), F32)
+                for other in range(3):
+                    slot = lax.rem(z - other + 4, 4)
+                    gone = gone + jnp.where(other < to, t_recv[s, slot, label, :], 0.0)
+                inside = within[s, jnp.maximum(to, 1), rows, :]
+                target[rows, :] = within[s, 0, rows, :] * jnp.exp(gone) + jnp.where(to > 0, inside, 0.0)
+            if d:
+                p_copies[s, d] = remote(
+                    target, chip_prefix.at[s, d], p_send_sems.at[s, d - 1], p_recv_sems.at[s, d - 1], z_peer[d]
+                )
 
     f_copies = {}
-    for d in (0, 1, 3, 2):
-        if d:
-            p_copies[d].wait_recv()
-        j = lax.rem(z - d + 4, 4)
-
-        def core(i, carry, d=d, j=j):
-            h = c * 24 + j * GROUP + i
-            rows = pl.ds(pl.multiple_of(i * HEAD, HEAD), HEAD)
-            first_total = jnp.where(zero_first, total_ref[pl.ds(h, 1), :], partner_total[pl.ds(h, 1), :])
-            first_state = jnp.where(zero_first, own_state[c, j, rows, :], partner_state[j, rows, :])
-            base = chip_prefix[d, rows, :]
-            full = base * jnp.exp(first_total) + first_state
-            prefix[c, j, rows, :] = jnp.where(zero_first, base, full)
-            f_send[j, rows, :] = jnp.where(zero_first, full, base)
-            return carry
-
-        lax.fori_loop(0, GROUP, core, 0, unroll=2)
-        copy = remote(f_send.at[j], prefix.at[c, j], f_send_sems.at[d], f_recv_sems.at[d], partner)
-        copy.start()
-        f_copies[d] = copy
+
+    def finish(s):
+        for d in (0, 1, 3, 2):
+            if d:
+                p_copies[s, d].wait_recv()
+            j = lax.rem(z - d + 4, 4)
+            for i in range(SUB):
+                h = c * 24 + s * 8 + j * SUB + i
+                rows = tile(j * SUB + i)
+                first_total = jnp.where(
+                    zero_first, total_ref[pl.ds(h, 1), :], partner_total[pl.ds(h, 1), :]
+                )
+                first_state = jnp.where(zero_first, own_state[c, s, rows, :], partner_state[s, rows, :])
+                base = chip_prefix[s, d, i * HEAD : (i + 1) * HEAD, :]
+                full = base * jnp.exp(first_total) + first_state
+                prefix[c, s, rows, :] = jnp.where(zero_first, base, full)
+                f_send[s, rows, :] = jnp.where(zero_first, full, base)
+        f_copies[s] = remote(f_send.at[s], prefix.at[c, s], f_send_sems.at[s], f_recv_sems.at[s], partner)
 
     square_ref[...] = jnp.zeros_like(square_ref)
 
-    def inter(half, j):
-        def one(i, carry):
-            h = half * 24 + j * GROUP + i
-            rows = pl.ds(pl.multiple_of(i * HEAD, HEAD), HEAD)
+    def inter(half, s):
+        def one(n, carry):
+            h = half * 24 + s * 8 + n
             across = jnp.broadcast_to(cum_ref[pl.ds(h, 1), :], (TOK, TOK)).T
-            high, low = parts(prefix[half, j, rows, :])
+            high, low = parts(prefix[half, s, tile(n), :])
             query = q_ref[:, columns(h)]
             out = attn_ref[:, columns(h)] + jnp.exp(across) * (dot(query, high) + dot(query, low))
             attn_ref[:, columns(h)] = out
             square_ref[...] += out * out
             return carry
 
-        lax.fori_loop(0, GROUP, one, 0, unroll=6)
-
-    for d in (0, 1, 3, 2):
-        inter(c, lax.rem(z - d + 4, 4))
-    for d in (0, 1, 3, 2):
-        f_copies[d].wait_recv()
-        inter(1 - c, lax.rem(z - d + 4, 4))
+        lax.fori_loop(0, 8, one, 0, unroll=8)
+
+    swaps = [swap(0)]
+    states(c, 0)
+    totals.wait_recv()
+    swaps[0].wait_recv()
+    join(0)
+    for s in (1, 2):
+        states(1 - c, s)
+        swaps.append(swap(s))
+        states(c, s)
+        swaps[s].wait_recv()
+        join(s)
+    loads[2].wait()
+    intra(0, 12)
+    row_sum(0)
+    intra(12, 24)
+    row_sum(1)
+    chip_prefixes(0)
+    intra(24, 36)
+    row_sum(2)
+    chip_prefixes(1)
+    intra(36, 48)
+    chip_prefixes(2)
+    for s in range(3):
+        finish(s)
+        inter(c, s)
+        f_copies[s].wait_recv()
+        inter(1 - c, s)
     loads[3].wait()
     scale = lax.rsqrt(jnp.sum(square_ref[...], axis=1, keepdims=True) * (1.0 / D) + 1e-6)
     scale = jnp.broadcast_to(scale, (TOK, HEAD))
@@ -306,9 +304,8 @@
         return carry
 
     lax.fori_loop(0, HEADS, norm, 0, unroll=6)
-    for copies in (ps_copies, t_copies, r_copies, p_copies, f_copies):
-        for copy in copies.values():
-            copy.wait_send()
+    for copy in copies:
+        copy.wait_send()
 
 
 def attention(queries, keys, values, resid, rate, attn_gain, moe_gain, select):
@@ -332,21 +329,21 @@
             pltpu.VMEM((HEADS, TOK), F32),
             pltpu.VMEM((HEADS, TOK), F32),
             pltpu.VMEM((HEADS, TOK), F32),
-            pltpu.VMEM((2, 4, ROWS, HEAD), F32),
-            pltpu.VMEM((4, ROWS, HEAD), F32),
+            pltpu.VMEM((2, 3, 4 * ROWS, HEAD), F32),
+            pltpu.VMEM((3, 4 * ROWS, HEAD), F32),
+            pltpu.VMEM((3, 3, MESSAGE, HEAD), F32),
+            pltpu.VMEM((3, 4, MESSAGE, HEAD), F32),
+            pltpu.VMEM((3, 4, ROWS, HEAD), F32),
             pltpu.VMEM((3, MESSAGE, HEAD), F32),
-            pltpu.VMEM((4, MESSAGE, HEAD), F32),
-            pltpu.VMEM((4, ROWS, HEAD), F32),
-            pltpu.VMEM((MESSAGE, HEAD), F32),
-            pltpu.VMEM((4, MESSAGE, HEAD), F32),
-            pltpu.VMEM((3, ROWS, HEAD), F32),
-            pltpu.VMEM((4, ROWS, HEAD), F32),
-            pltpu.VMEM((4, ROWS, HEAD), F32),
-            pltpu.VMEM((2, 4, ROWS, HEAD), F32),
+            pltpu.VMEM((3, 4, MESSAGE, HEAD), F32),
+            pltpu.VMEM((3, 3, ROWS, HEAD), F32),
+            pltpu.VMEM((3, 4, ROWS, HEAD), F32),
+            pltpu.VMEM((3, 4 * ROWS, HEAD), F32),
+            pltpu.VMEM((2, 3, 4 * ROWS, HEAD), F32),
             pltpu.VMEM((TOK, D), F32),
             pltpu.VMEM((TOK, HEAD), F32),
-            dma((4,)), dma((2,)), dma((4,)), dma((4,)), dma((3,)), dma((3,)),
-            dma((3,)), dma((3,)), dma((3,)), dma((3,)), dma((4,)), dma((4,)),
+            dma((4,)), dma((2,)), dma((3,)), dma((3,)), dma((3, 3)), dma((3, 3)),
+            dma((3, 3)), dma((3, 3)), dma((3, 3)), dma((3, 3)), dma((3,)), dma((3,)),
         ],
         compiler_params=pltpu.CompilerParams(
             collective_id=0, has_side_effects=True, vmem_limit_bytes=56 * 2**20

time: 169 us -> 146 us (0.86)
  Pallas kernels: 161 us -> 139 us
    pallas_call x1, Pallas kernels: 75.7 us -> 52.6 us  [attention(): pl.pallas_call(attention_kernel, out_shape=(jax.ShapeDtypeStruct((TOK, D)...]
where the time goes in v4:
time: 146 us
  Pallas kernels  139 us (95%)
  local copies, waits for them, and re-layouts  3.81 us (3%)
  other arithmetic  3.12 us (2%)
    pallas_call x1, Pallas kernels, window(): pl.pallas_call(window_kernel, out_shape=jax.ShapeDtypeStruct((TOK, D), BF...  86.4 us
    pallas_call x1, Pallas kernels, attention(): pl.pallas_call(attention_kernel, out_shape=(jax.ShapeDtypeStruct((TOK, D)...  52.6 us
    unnamed x2, local copies, waits for them, and re-layouts  3.47 us

profile of v4, /device:TPU:0, one launch (start us, length us, event | category | flops | bytes accessed | tf_op | source)
XLA Modules:
  0.0 146.2 jit_solution(10089496839337890987)
XLA Ops:
  0.0 0.7 compare_bitcast_fusion
  0.7 0.8 copy.18
  1.5 0.1 eq.37
  1.6 0.2 fusion
  1.8 0.1 convert_element_type.33
  2.0 0.1 copy.20
  2.1 0.6 fusion.7.select_ref
  2.7 0.8 multiply_reduce_fusion
  3.6 0.1 fusion.3
  3.7 0.1 fusion.4
  3.8 0.7 pad_maximum_fusion.mixing_ref
  4.5 52.6 %attention.1 = (bf16[128,6144]{1,0:T(8,128)(2,1)}, bf16[64,6144]{1,0:T(8,128)(2,1)}, bf16[64,6144]{1,0:T(8,128)(2,1)}) custom-call(bf16[128,6144]{1,0:T(8,128)(2,1)} %bitcast.28, bf16[128,6144]{1,0:T(8,128)(2,1)} %bitcast.29, bf16[128,6144]{1,0:T(8,128)(2,1)} %bitcast.30, bf16[128,6144]{1,0:T(8,128)(2,1)} %bitcast.31, f32[48,128]{1,0:T(8,128)} %bitcast.32, ...), custom_call_target="tpu_custom_call" | custom-call | tf_op jit(solution)/shard_map/attention/pallas_call | solution.py:315
  57.1 86.4 %window.1 = bf16[128,6144]{1,0:T(8,128)(2,1)} custom-call(bf16[64,6144]{1,0:T(8,128)(2,1)} %get-tuple-element.8.outbox_ref, bf16[128,6144]{1,0:T(8,128)(2,1)} %get-tuple-element.9.high_ref, bf16[64,6144]{1,0:T(8,128)(2,1)} %get-tuple-element.10.low_ref, f32[128,128]{1,0:T(8,128)} %pad_maximum_fusion.mixing_ref, bf16[6144,640]{1,0:T(8,128)(2,1)} %bitcast.25, ...), custom_call_target="tpu_custom_call" | custom-call | tf_op jit(solution)/shard_map/window/pallas_call | solution.py:596
  143.5 2.7 %copy.23 = bf16[1,128,6144]{2,1,0:T(8,128)(2,1)} copy(bf16[1,128,6144]{2,1,0:T(8,128)(2,1)} %bitcast.27) | data formatting | bytes 3145728
  (3 shorter events, 0.0 us)

commit v5 on v4

v5 whole, which is shorter than its diff:
```python
import jax
import jax.numpy as jnp
from jax import lax
from jax.experimental import pallas as pl
from jax.experimental.pallas import tpu as pltpu
from jax.sharding import PartitionSpec as P

D = 6144
HEADS = 48
HEAD = 128
TOK = 128
CAP = 16
FLY = 4
SUB = 2
ROWS = SUB * HEAD
MESSAGE = ROWS + 8
BF = jnp.bfloat16
F32 = jnp.float32
HIGH = lax.Precision.HIGHEST


def dot(a, b):
    return jnp.dot(a, b, preferred_element_type=F32)


def dot_t(a, b):
    return lax.dot_general(a, b, (((1,), (1,)), ((), ())), preferred_element_type=F32)


def parts(x):
    high = x.astype(BF)
    return high, (x - high.astype(F32)).astype(BF)


def place():
    me = lax.axis_index("ctx")
    return me // 8, lax.rem(me // 2, 4), lax.rem(me, 2)


def index_of(y, z, c):
    return (y * 4 + z) * 2 + c


def columns(h):
    return pl.ds(pl.multiple_of(h * HEAD, HEAD), HEAD)


BLOCK = 4 * CAP
STEP = 1024
UNITS = 640
CHUNKS = 3
PAIR = 2 * CAP
WIDE = D // CHUNKS
NARROW = 512


def scan_attention(
    where, barrier,
    q_hbm, k_hbm, v_hbm, resid_hbm, rate_ref, attn_gain_ref, moe_gain_ref, experts_ref, combine_ref,
    high_ref, low_ref, outbox_ref, mixing_ref,
    partner_total, partner_state, t_recv, r_recv, chip_prefix, prefix,
    load_sems, small_sems, ps_send_sems, ps_recv_sems, t_send_sems, t_recv_sems,
    r_send_sems, r_recv_sems, p_send_sems, p_recv_sems, f_send_sems, f_recv_sems,
    q_ref, k_ref, v_ref, resid_ref, cum_ref, total_ref, own_state,
    t_send, within, r_send, p_send, f_send, attn_ref, square_ref, select_ref,
):
    y, z, c = where
    loads = [
        pltpu.make_async_copy(a, b, load_sems.at[i])
        for i, (a, b) in enumerate(
            ((k_hbm, k_ref), (v_hbm, v_ref), (q_hbm, q_ref), (resid_hbm, resid_ref))
        )
    ]
    for load in loads:
        load.start()
    partner = index_of(y, z, 1 - c)
    z_peer = [index_of(y, lax.rem(z + d, 4), c) for d in range(4)]
    y_peer = [index_of(lax.rem(y + d, 4), z, c) for d in range(4)]
    rate = rate_ref[...]
    earlier = lax.broadcasted_iota(jnp.int32, (TOK, TOK), 0)
    later = lax.broadcasted_iota(jnp.int32, (TOK, TOK), 1)
    cum_ref[...] = jnp.dot(
        rate, (earlier <= later).astype(F32), precision=HIGH, preferred_element_type=F32
    )
    total_ref[...] = jnp.dot(
        rate, jnp.ones((TOK, TOK), F32), precision=HIGH, preferred_element_type=F32
    )
    copies = []

    def remote(src, dst, send_sem, recv_sem, peer):
        copy = pltpu.make_async_remote_copy(
            src_ref=src, dst_ref=dst, send_sem=send_sem, recv_sem=recv_sem, device_id={"ctx": peer}
        )
        copy.start()
        copies.append(copy)
        return copy

    def tile(i):
        return pl.ds(pl.multiple_of(i * HEAD, HEAD), HEAD)

    def state_of(h):
        row = jnp.exp(total_ref[pl.ds(h, 1), :] - cum_ref[pl.ds(h, 1), :])
        keys = k_ref[:, columns(h)].astype(F32).T * row
        high, low = parts(keys)
        values = v_ref[:, columns(h)]
        return dot(high, values) + dot(low, values)

    def states(half, s):
        def one(n, carry):
            own_state[half, s, tile(n), :] = state_of(half * 24 + s * 8 + n)
            return carry

        lax.fori_loop(0, 8, one, 0, unroll=8)

    loads[0].wait()
    loads[1].wait()
    states(1 - c, 0)
    pl.semaphore_wait(barrier, 15)
    totals = remote(total_ref, partner_total, small_sems.at[0], small_sems.at[1], partner)
    zero_first = c == 0

    def swap(s):
        return remote(
            own_state.at[1 - c, s], partner_state.at[s], ps_send_sems.at[s], ps_recv_sems.at[s], partner
        )

    order = (2, 1, 3, 0)
    t_copies = {}

    def join(s):
        for d in order:
            j = lax.rem(z + d, 4)
            target = t_recv.at[s, 0] if d == 0 else t_send.at[s, d - 1]
            for i in range(SUB):
                h = c * 24 + s * 8 + j * SUB + i
                rows = tile(j * SUB + i)
                mine = total_ref[pl.ds(h, 1), :]
                other = partner_total[pl.ds(h, 1), :]
                keep = jnp.exp(jnp.where(zero_first, other, 0.0))
                take = jnp.exp(jnp.where(zero_first, 0.0, mine))
                target[i * HEAD : (i + 1) * HEAD, :] = (
                    keep * own_state[c, s, rows, :] + take * partner_state[s, rows, :]
                )
                target[ROWS + i : ROWS + i + 1, :] = mine + other
            target[ROWS + SUB :, :] = jnp.zeros((8 - SUB, HEAD), F32)
            if d:
                t_copies[s, d] = remote(
                    target, t_recv.at[s, d], t_send_sems.at[s, d - 1], t_recv_sems.at[s, d - 1], z_peer[d]
                )

    lower = earlier >= later

    def intra(first, last):
        def one(h, carry):
            across = jnp.broadcast_to(cum_ref[pl.ds(h, 1), :], (TOK, TOK))
            weights = jnp.exp(jnp.where(lower, across.T - across, -1e30))
            scores = dot_t(q_ref[:, columns(h)], k_ref[:, columns(h)]) * weights
            high, low = parts(scores)
            values = v_ref[:, columns(h)]
            attn_ref[:, columns(h)] = dot(high, values) + dot(low, values)
            return carry

        lax.fori_loop(first, last, one, 0, unroll=6)

    r_copies = {}

    def row_sum(s):
        for d in (1, 3, 2):
            t_copies[s, d].wait_recv()
        for i in range(SUB):
            rows = slice(i * HEAD, (i + 1) * HEAD)
            label = slice(ROWS + i, ROWS + i + 1)
            state = t_recv[s, z, rows, :]
            within[s, 1, rows, :] = state
            for other in range(1, 4):
                slot = lax.rem(z - other + 4, 4)
                state = state * jnp.exp(t_recv[s, slot, label, :]) + t_recv[s, slot, rows, :]
                if other < 3:
                    within[s, other + 1, rows, :] = state
            r_send[s, rows, :] = state
            r_send[s, label, :] = (
                t_recv[s, 0, label, :] + t_recv[s, 1, label, :]
                + t_recv[s, 2, label, :] + t_recv[s, 3, label, :]
            )
        r_send[s, ROWS + SUB :, :] = jnp.zeros((8 - SUB, HEAD), F32)
        for d in (2, 1, 3):
            r_copies[s, d] = remote(
                r_send.at[s], r_recv.at[s, d], r_send_sems.at[s, d - 1], r_recv_sems.at[s, d - 1], y_peer[d]
            )
        r_recv[s, 0] = r_send[s]

    p_copies = {}

    def chip_prefixes(s):
        for d in (1, 3, 2):
            r_copies[s, d].wait_recv()
        for i in range(SUB):
            rows = slice(i * HEAD, (i + 1) * HEAD)
            label = slice(ROWS + i, ROWS + i + 1)
            state = jnp.zeros((HEAD, HEAD), F32)
            for other in range(3):
                slot = lax.rem(y - other + 4, 4)
                joined = state * jnp.exp(r_recv[s, slot, label, :]) + r_recv[s, slot, rows, :]
                state = jnp.where(other < y, joined, state)
            within[s, 0, rows, :] = state
        for d in order:
            to = lax.rem(z + d, 4)
            target = chip_prefix.at[s, 0] if d == 0 else p_send.at[s, d - 1]
            for i in range(SUB):
                rows = slice(i * HEAD, (i + 1) * HEAD)
                label = slice(ROWS + i, ROWS + i + 1)
                gone = jnp.zeros((1, HEAD), F32)
                for other in range(3):
                    slot = lax.rem(z - other + 4, 4)
                    gone = gone + jnp.where(other < to, t_recv[s, slot, label, :], 0.0)
                inside = within[s, jnp.maximum(to, 1), rows, :]
                target[rows, :] = within[s, 0, rows, :] * jnp.exp(gone) + jnp.where(to > 0, inside, 0.0)
            if d:
                p_copies[s, d] = remote(
                    target, chip_prefix.at[s, d], p_send_sems.at[s, d - 1], p_recv_sems.at[s, d - 1], z_peer[d]
                )

    f_copies = {}

    def finish(s):
        for d in (0, 1, 3, 2):
            if d:
                p_copies[s, d].wait_recv()
            j = lax.rem(z - d + 4, 4)
            for i in range(SUB):
                h = c * 24 + s * 8 + j * SUB + i
                rows = tile(j * SUB + i)
                first_total = jnp.where(
                    zero_first, total_ref[pl.ds(h, 1), :], partner_total[pl.ds(h, 1), :]
                )
                first_state = jnp.where(zero_first, own_state[c, s, rows, :], partner_state[s, rows, :])
                base = chip_prefix[s, d, i * HEAD : (i + 1) * HEAD, :]
                full = base * jnp.exp(first_total) + first_state
                prefix[c, s, rows, :] = jnp.where(zero_first, base, full)
                f_send[s, rows, :] = jnp.where(zero_first, full, base)
        f_copies[s] = remote(f_send.at[s], prefix.at[c, s], f_send_sems.at[s], f_recv_sems.at[s], partner)

    square_ref[...] = jnp.zeros_like(square_ref)

    def tables():
        expert, slot = later // CAP, lax.rem(later, CAP)
        chosen = [
            jnp.broadcast_to(experts_ref[j : j + 1, :].astype(F32), (TOK, TOK)).T for j in range(2)
        ]
        weight = [jnp.broadcast_to(combine_ref[j : j + 1, :], (TOK, TOK)).T for j in range(2)]
        window = later < FLY * CAP
        named = [(one == expert.astype(F32)) & window for one in chosen]
        either = named[0] | named[1]
        ahead = dot((earlier > later).astype(F32).astype(BF), either.astype(F32).astype(BF))
        match = either & (ahead == slot.astype(F32))
        found = match.astype(F32)
        select_ref[...] = found.T[: FLY * CAP, :].astype(BF)
        first = jnp.where(chosen[0] < FLY, named[0].astype(F32), named[1].astype(F32))
        mixing_ref[:TOK, :] = first * found
        mixing_ref[TOK:, :] = jnp.where(named[0], weight[0], weight[1]) * found

    def inter(half, s):
        def one(n, carry):
            h = half * 24 + s * 8 + n
            across = jnp.broadcast_to(cum_ref[pl.ds(h, 1), :], (TOK, TOK)).T
            high, low = parts(prefix[half, s, tile(n), :])
            query = q_ref[:, columns(h)]
            out = attn_ref[:, columns(h)] + jnp.exp(across) * (dot(query, high) + dot(query, low))
            attn_ref[:, columns(h)] = out
            square_ref[...] += out * out
            return carry

        lax.fori_loop(0, 8, one, 0, unroll=8)

    swaps = [swap(0)]
    states(c, 0)
    totals.wait_recv()
    swaps[0].wait_recv()
    join(0)
    for s in (1, 2):
        states(1 - c, s)
        swaps.append(swap(s))
        states(c, s)
        swaps[s].wait_recv()
        join(s)
    loads[2].wait()
    tables()
    intra(0, 12)
    row_sum(0)
    intra(12, 24)
    row_sum(1)
    chip_prefixes(0)
    intra(24, 36)
    row_sum(2)
    chip_prefixes(1)
    intra(36, 48)
    chip_prefixes(2)
    for s in range(3):
        finish(s)
        inter(c, s)
        f_copies[s].wait_recv()
        inter(1 - c, s)
    loads[3].wait()
    scale = lax.rsqrt(jnp.sum(square_ref[...], axis=1, keepdims=True) * (1.0 / D) + 1e-6)
    scale = jnp.broadcast_to(scale, (TOK, HEAD))
    square_ref[...] = jnp.zeros_like(square_ref)

    def residual(h, carry):
        out = resid_ref[:, columns(h)].astype(F32) + attn_ref[:, columns(h)] * scale * attn_gain_ref[:, columns(h)]
        attn_ref[:, columns(h)] = out
        square_ref[...] += out * out
        return carry

    lax.fori_loop(0, HEADS, residual, 0, unroll=6)
    scale_2 = lax.rsqrt(jnp.sum(square_ref[...], axis=1, keepdims=True) * (1.0 / D) + 1e-6)
    scale_2 = jnp.broadcast_to(scale_2, (TOK, HEAD))
    select = select_ref[...]

    def norm(h, carry):
        out = attn_ref[:, columns(h)]
        high, low = parts(out)
        high_ref[:, columns(h)] = high
        low_ref[:, columns(h)] = dot(select, low).astype(BF)
        normed = (out * scale_2 * moe_gain_ref[:, columns(h)]).astype(BF)
        outbox_ref[:, columns(h)] = dot(select, normed).astype(BF)
        return carry

    lax.fori_loop(0, HEADS, norm, 0, unroll=6)
    for copy in copies:
        copy.wait_send()


def expert_window(
    where,
    outbox_ref, high_ref, low_ref, mixing_ref, up_hbm, down_hbm,
    high_in, low_in, mixing_in, sums_ref,
    rows_ref, partner_part, relay_in, near_in, far_in,
    load_sems, y_send, y_recv, core_send, core_recv, z_send, z_recv, hop_send, hop_recv,
    part_send, part_recv, ring_send, ring_recv, next_send, next_recv, sums_send, sums_recv,
    up_ref, down_ref, total_ref, hidden_ref, part_ref, sum_ref, relay_out, final_ref,
):
    y, z, c = where
    section = lax.axis_index("section")
    after = lax.rem(section + 1, 4)
    before = lax.rem(section + 3, 4)
    loads = [
        pltpu.make_async_copy(up_hbm, up_ref, load_sems.at[0]),
        pltpu.make_async_copy(down_hbm, down_ref, load_sems.at[1]),
    ]
    for load in loads:
        load.start()
    partner = index_of(y, z, 1 - c)
    plus, minus = index_of(y, lax.rem(z + 1, 4), c), index_of(y, lax.rem(z + 3, 4), c)
    y_peer = [index_of(lax.rem(y + d, 4), z, c) for d in range(4)]
    sent = []

    def send(src, dst, send_sem, recv_sem, peer, section_to=None):
        target = {"ctx": peer} if section_to is None else {"section": section_to, "ctx": peer}
        copy = pltpu.make_async_remote_copy(
            src_ref=src, dst_ref=dst, send_sem=send_sem, recv_sem=recv_sem, device_id=target
        )
        copy.start()
        sent.append(copy)

    def arrived(dst, recv_sem, peer, section_to=None):
        target = {"ctx": peer} if section_to is None else {"section": section_to, "ctx": peer}
        pltpu.make_async_remote_copy(
            src_ref=dst, dst_ref=dst, send_sem=recv_sem, recv_sem=recv_sem, device_id=target
        ).wait_recv()

    spot = (0, 1, 3, 2)

    def piece(block, core, p):
        row = p // 2 * 4 * BLOCK + block * BLOCK + core * PAIR + p % 2 * CAP
        return rows_ref.at[pl.ds(pl.multiple_of(row, CAP), CAP), :]

    def box(e):
        return pl.ds(pl.multiple_of(e * CAP, CAP), CAP)

    def to_column(d):
        send(
            outbox_ref.at[box(lax.rem(y + d, 4)), :], piece(0, c, spot[d]),
            y_send.at[d - 1], y_recv.at[d - 1], y_peer[d],
        )

    to_column(1)
    to_column(3)
    rows_ref[pl.ds(pl.multiple_of(c * PAIR, CAP), CAP), :] = outbox_ref[box(y), :]

    def spread(p):
        src = piece(0, c, p)
        send(src, piece(1, c, p), z_send.at[0, p], z_recv.at[0, p], plus)
        send(src, piece(2, c, p), z_send.at[1, p], z_recv.at[1, p], minus)
        send(src, src, core_send.at[0, p], core_recv.at[0, p], partner)

    def from_minus(p):
        src = piece(1, c, p)
        arrived(src, z_recv.at[0, p], minus)
        if p % 2 == 0:
            send(src, piece(3, c, p), hop_send.at[p], hop_recv.at[p], plus)
        send(src, src, core_send.at[1, p], core_recv.at[1, p], partner)

    def from_plus(p):
        src = piece(2, c, p)
        arrived(src, z_recv.at[1, p], plus)
        if p % 2 == 1:
            send(src, piece(3, c, p), hop_send.at[p], hop_recv.at[p], minus)
        send(src, src, core_send.at[2, p], core_recv.at[2, p], partner)

    def from_far(p):
        src = piece(3, c, p)
        arrived(src, hop_recv.at[p], plus if p % 2 else minus)
        send(src, src, core_send.at[3, p], core_recv.at[3, p], partner)

    def from_column(d):
        arrived(piece(0, c, spot[d]), y_recv.at[d - 1], y_peer[4 - d])
        spread(spot[d])

    def up(g):
        first, count = g * 4 * BLOCK, 4 * BLOCK
        for block in range(4):
            for p in (2 * g, 2 * g + 1):
                arrived(piece(block, 1 - c, p), core_recv.at[block, p], partner)
        total_ref[...] = jnp.zeros_like(total_ref)

        def one(i, carry):
            at = pl.ds(pl.multiple_of(i * STEP, STEP), STEP)
            total_ref[...] += dot(rows_ref[first : first + count, at], up_ref[at, :])
            return carry

        lax.fori_loop(0, D // STEP, one, 0)
        hidden_ref[first : first + count, :] = jax.nn.gelu(total_ref[...], approximate=True).astype(BF)

    def down(g, q):
        first = g * 4 * BLOCK

        def one(i, carry):
            at = pl.ds(pl.multiple_of(i * NARROW, NARROW), NARROW)
            from_at = pl.ds(pl.multiple_of(q * WIDE + i * NARROW, NARROW), NARROW)
            out = dot(hidden_ref[first : first + 4 * BLOCK, :], down_ref[:, from_at]).astype(BF)
            for block in range(4):
                for core in range(2):
                    row = block * BLOCK + core * PAIR
                    part_ref[g, q, core, block * PAIR : (block + 1) * PAIR, at] = out[row : row + PAIR, :]
            return carry

        lax.fori_loop(0, WIDE // NARROW, one, 0)
        send(
            part_ref.at[g, q, 1 - c], partner_part.at[g, q], part_send.at[g, q], part_recv.at[g, q], partner
        )

    def over_columns(body):
        def one(i, carry):
            body(pl.ds(pl.multiple_of(i * NARROW, NARROW), NARROW))
            return carry

        lax.fori_loop(0, WIDE // NARROW, one, 0)

    def share(g, q, block, i):
        first = block * PAIR + i * CAP
        return sum_ref.at[g, q, first : first + CAP, :]

    def core_sum(g, q):
        arrived(partner_part.at[g, q], part_recv.at[g, q], partner)

        def add(at):
            sum_ref[g, q, :, at] = (
                part_ref[g, q, c, :, at].astype(F32) + partner_part[g, q, :, at].astype(F32)
            ).astype(BF)

        over_columns(add)
        out, back = ring_send.at[g, q], ring_recv.at[g, q]
        send(share(g, q, 3, 0), relay_in.at[g, q, 0], out.at[2], back.at[2], plus)
        send(share(g, q, 3, 1), relay_in.at[g, q, 1], out.at[3], back.at[3], minus)
        send(share(g, q, 2, 1), near_in.at[g, q, 0], out.at[0], back.at[0], plus)
        send(share(g, q, 1, 0), near_in.at[g, q, 1], out.at[1], back.at[1], minus)

    def relay(g, q):
        for side in range(2):
            arrived(relay_in.at[g, q, side], ring_recv.at[g, q, 2 + side], (minus, plus)[side])
            mine = share(g, q, 2 - side, side)

            def add(at, side=side, mine=mine):
                relay_out[g, q, side, :, at] = (
                    mine[:, at].astype(F32) + relay_in[g, q, side, :, at].astype(F32)
                ).astype(BF)

            over_columns(add)
            send(
                relay_out.at[g, q, side], far_in.at[g, q, side],
                ring_send.at[g, q, 4 + side], ring_recv.at[g, q, 4 + side], (plus, minus)[side],
            )

    def final(g, q):
        arrived(near_in.at[g, q, 0], ring_recv.at[g, q, 0], minus)
        arrived(near_in.at[g, q, 1], ring_recv.at[g, q, 1], plus)
        arrived(far_in.at[g, q, 0], ring_recv.at[g, q, 4], minus)
        arrived(far_in.at[g, q, 1], ring_recv.at[g, q, 5], plus)
        for i in range(2):
            mine = share(g, q, 0, i)
            p = 2 * g + i

            def add(at, i=i, p=p, mine=mine):
                final_ref[q, p * CAP : (p + 1) * CAP, at] = (
                    mine[:, at].astype(F32)
                    + near_in[g, q, 1 - i, :, at].astype(F32)
                    + far_in[g, q, i, :, at].astype(F32)
                ).astype(BF)

            over_columns(add)
            d = spot[p]
            send(
                final_ref.at[q, p * CAP : (p + 1) * CAP, :], sums_ref.at[box(y), q * WIDE : (q + 1) * WIDE],
                sums_send.at[q, d], sums_recv.at[q, d], y_peer[(4 - d) % 4], after,
            )

    spread(0)
    send(high_ref, high_in, next_send.at[0], next_recv.at[0], y_peer[0], after)
    send(low_ref, low_in, next_send.at[1], next_recv.at[1], y_peer[0], after)
    send(mixing_ref, mixing_in, next_send.at[2], next_recv.at[2], y_peer[0], after)
    from_column(1)
    to_column(2)
    from_column(3)
    from_minus(0)
    from_plus(0)
    from_column(2)
    from_minus(1)
    from_plus(1)
    from_far(0)
    from_far(1)
    loads[0].wait()
    up(0)
    for p in (2, 3):
        from_minus(p)
        from_plus(p)
    loads[1].wait()
    down(0, 0)
    down(0, 1)
    core_sum(0, 0)
    down(0, 2)
    core_sum(0, 1)
    core_sum(0, 2)
    from_far(2)
    from_far(3)
    up(1)
    for q in range(CHUNKS):
        relay(0, q)
    down(1, 0)
    down(1, 1)
    core_sum(1, 0)
    down(1, 2)
    core_sum(1, 1)
    final(0, 0)
    core_sum(1, 2)
    final(0, 1)
    relay(1, 0)
    final(0, 2)
    relay(1, 1)
    final(1, 0)
    relay(1, 2)
    arrived(high_in, next_recv.at[0], y_peer[0], before)
    arrived(low_in, next_recv.at[1], y_peer[0], before)
    arrived(mixing_in, next_recv.at[2], y_peer[0], before)
    final(1, 1)
    final(1, 2)
    for q in range(CHUNKS):
        for d in range(4):
            arrived(sums_ref.at[0:CAP, q * WIDE : (q + 1) * WIDE], sums_recv.at[q, d], y_peer[d], before)
    for copy in sent:
        copy.wait_send()


def layer_kernel(
    q_hbm, k_hbm, v_hbm, resid_hbm, rate_ref, attn_gain_ref, moe_gain_ref, experts_ref, combine_ref,
    up_hbm, down_hbm,
    high_in, low_in, mixing_in, sums_ref,
    high_ref, low_ref, outbox_ref, mixing_ref,
    partner_total, partner_state, t_recv, r_recv, chip_prefix, prefix,
    rows_ref, partner_part, relay_in, near_in, far_in,
    *sems,
):
    y, z, c = place()
    section = lax.axis_index("section")
    barrier = pltpu.get_barrier_semaphore()
    ring = [index_of(y, lax.rem(z + d, 4), c) for d in (1, 2, 3)]
    column = [index_of(lax.rem(y + d, 4), z, c) for d in range(4)]
    for peer in [index_of(y, z, 1 - c)] + ring + column[1:]:
        pl.semaphore_signal(barrier, inc=1, device_id={"ctx": peer})
    for step in (1, 3):
        for peer in column:
            pl.semaphore_signal(
                barrier, inc=1, device_id={"section": lax.rem(section + step, 4), "ctx": peer}
            )

    def first(*local_refs):
        scan_attention(
            (y, z, c), barrier,
            q_hbm, k_hbm, v_hbm, resid_hbm, rate_ref, attn_gain_ref, moe_gain_ref, experts_ref, combine_ref,
            high_ref, low_ref, outbox_ref, mixing_ref,
            partner_total, partner_state, t_recv, r_recv, chip_prefix, prefix,
            *sems[:12], *local_refs,
        )

    pl.run_scoped(
        first,
        pltpu.VMEM((TOK, D), BF),
        pltpu.VMEM((TOK, D), BF),
        pltpu.VMEM((TOK, D), BF),
        pltpu.VMEM((TOK, D), BF),
        pltpu.VMEM((HEADS, TOK), F32),
        pltpu.VMEM((HEADS, TOK), F32),
        pltpu.VMEM((2, 3, 4 * ROWS, HEAD), F32),
        pltpu.VMEM((3, 3, MESSAGE, HEAD), F32),
        pltpu.VMEM((3, 4, ROWS, HEAD), F32),
        pltpu.VMEM((3, MESSAGE, HEAD), F32),
        pltpu.VMEM((3, 3, ROWS, HEAD), F32),
        pltpu.VMEM((3, 4 * ROWS, HEAD), F32),
        pltpu.VMEM((TOK, D), F32),
        pltpu.VMEM((TOK, HEAD), F32),
        pltpu.VMEM((FLY * CAP, TOK), BF),
    )

    def second(*local_refs):
        expert_window(
            (y, z, c), outbox_ref, high_ref, low_ref, mixing_ref, up_hbm, down_hbm,
            high_in, low_in, mixing_in, sums_ref,
            rows_ref, partner_part, relay_in, near_in, far_in,
            *sems[12:], *local_refs,
        )

    pl.run_scoped(
        second,
        pltpu.VMEM((D, UNITS), BF),
        pltpu.VMEM((UNITS, D), BF),
        pltpu.VMEM((4 * BLOCK, UNITS), F32),
        pltpu.VMEM((8 * BLOCK, UNITS), BF),
        pltpu.VMEM((2, CHUNKS, 2, 4 * PAIR, WIDE), BF),
        pltpu.VMEM((2, CHUNKS, 4 * PAIR, WIDE), BF),
        pltpu.VMEM((2, CHUNKS, 2, CAP, WIDE), BF),
        pltpu.VMEM((CHUNKS, BLOCK, WIDE), BF),
    )


def layer(queries, keys, values, resid, rate, attn_gain, moe_gain, experts, combine, w_up, w_down):
    vmem = pl.BlockSpec(memory_space=pltpu.VMEM)
    hbm = pl.BlockSpec(memory_space=pl.ANY)
    dma = pltpu.SemaphoreType.DMA
    return pl.pallas_call(
        layer_kernel,
        out_shape=(
            jax.ShapeDtypeStruct((TOK, D), BF),
            jax.ShapeDtypeStruct((BLOCK, D), BF),
            jax.ShapeDtypeStruct((2 * TOK, TOK), F32),
            jax.ShapeDtypeStruct((BLOCK, D), BF),
        ),
        in_specs=[hbm] * 4 + [vmem] * 5 + [hbm] * 2,
        out_specs=(hbm, hbm, hbm, hbm),
        scratch_shapes=[
            pltpu.VMEM((TOK, D), BF),
            pltpu.VMEM((BLOCK, D), BF),
            pltpu.VMEM((BLOCK, D), BF),
            pltpu.VMEM((2 * TOK, TOK), F32),
            pltpu.VMEM((HEADS, TOK), F32),
            pltpu.VMEM((3, 4 * ROWS, HEAD), F32),
            pltpu.VMEM((3, 4, MESSAGE, HEAD), F32),
            pltpu.VMEM((3, 4, MESSAGE, HEAD), F32),
            pltpu.VMEM((3, 4, ROWS, HEAD), F32),
            pltpu.VMEM((2, 3, 4 * ROWS, HEAD), F32),
            pltpu.VMEM((8 * BLOCK, D), BF),
            pltpu.VMEM((2, CHUNKS, 4 * PAIR, WIDE), BF),
            pltpu.VMEM((2, CHUNKS, 2, CAP, WIDE), BF),
            pltpu.VMEM((2, CHUNKS, 2, CAP, WIDE), BF),
            pltpu.VMEM((2, CHUNKS, 2, CAP, WIDE), BF),
            dma((4,)), dma((2,)), dma((3,)), dma((3,)), dma((3, 3)), dma((3, 3)),
            dma((3, 3)), dma((3, 3)), dma((3, 3)), dma((3, 3)), dma((3,)), dma((3,)),
            dma((2,)), dma((3,)), dma((3,)), dma((4, 4)), dma((4, 4)), dma((2, 4)), dma((2, 4)),
            dma((4,)), dma((4,)), dma((2, CHUNKS)), dma((2, CHUNKS)),
            dma((2, CHUNKS, 6)), dma((2, CHUNKS, 6)),
            dma((3,)), dma((3,)), dma((CHUNKS, 4)), dma((CHUNKS, 4)),
        ],
        compiler_params=pltpu.CompilerParams(
            collective_id=0, has_side_effects=True, vmem_limit_bytes=60 * 2**20
        ),
        name="layer",
    )(queries, keys, values, resid, rate, attn_gain, moe_gain, experts, combine, w_up, w_down)


def mix_kernel(high_ref, low_ref, mixing_ref, sums_ref, out_ref):
    first = mixing_ref[:TOK, :BLOCK].astype(BF)
    weight_high, weight_low = parts(mixing_ref[TOK:, :BLOCK])
    for i in range(D // 2 // NARROW):
        at = slice(i * NARROW, (i + 1) * NARROW)
        sums = sums_ref[:, at]
        mixed = dot(weight_high, sums) + dot(weight_low, sums)
        out_ref[:, at] = ((high_ref[:, at].astype(F32) + dot(first, low_ref[:, at])) + mixed).astype(BF)


def mix(high, low, mixing, sums):
    wide = D // 2
    return pl.pallas_call(
        mix_kernel,
        out_shape=jax.ShapeDtypeStruct((TOK, D), BF),
        grid=(D // wide,),
        in_specs=[
            pl.BlockSpec((TOK, wide), lambda i: (0, i)),
            pl.BlockSpec((BLOCK, wide), lambda i: (0, i)),
            pl.BlockSpec((2 * TOK, TOK), lambda i: (0, 0)),
            pl.BlockSpec((BLOCK, wide), lambda i: (0, i)),
        ],
        out_specs=pl.BlockSpec((TOK, wide), lambda i: (0, i)),
        compiler_params=pltpu.CompilerParams(vmem_limit_bytes=32 * 2**20),
        name="mix",
    )(high, low, mixing, sums)


def local(
    resid, queries, keys, values, log_decay, attn_gain, moe_gain, experts, combine_weight, w_up, w_down
):
    high, low, mixing, sums = layer(
        queries[0], keys[0], values[0], resid[0], log_decay[0].T, attn_gain, moe_gain,
        experts[0].T, combine_weight[0].T, w_up[0], w_down[0],
    )
    return mix(high, low, mixing, sums)[None]


def solution(mesh):
    token = P("section", "ctx", None)
    return jax.shard_map(
        local,
        mesh=mesh,
        in_specs=(
            token, token, token, token, token,
            P("section", None), P("section", None),
            token, token,
            P("section", None, "ctx"), token,
        ),
        out_specs=token,
        check_vma=False,
    )
```

time: 146 us -> 137 us (0.938)
  Pallas kernels: 139 us -> 132 us
  other arithmetic: 3.12 us -> 0 us
    pallas_call x2, Pallas kernels: 139 us -> 132 us  [the longest x1 129 us: layer(): pl.pallas_call(layer_kernel, out_shape=(jax.ShapeDtypeStruct((TOK, D), BF...]
    reduce_sum x2 -> x0, other arithmetic: 1.49 us -> none  [the longest x1 0.85 us: local(): weighted = (pairs * combine_weight[0][:, :, None]).sum(axis=1)]
    unnamed x2 -> x8, local copies, waits for them, and re-layouts: 3.47 us -> 4.57 us
where the time goes in v5:
time: 137 us; the launch traced here: 136 us
  Pallas kernels  132 us (96%)
  local copies, waits for them, and re-layouts  4.57 us (3%)
    pallas_call x1, Pallas kernels, layer(): pl.pallas_call(layer_kernel, out_shape=(jax.ShapeDtypeStruct((TOK, D), BF...  129 us
    unnamed x8, local copies, waits for them, and re-layouts  4.57 us

profile of v5, /device:TPU:0, one launch (start us, length us, event | category | flops | bytes accessed | tf_op | source)
XLA Modules:
  0.0 136.4 jit_solution(17825451690428052683)
XLA Ops:
  0.0 129.1 %layer.1 = (bf16[128,6144]{1,0:T(8,128)(2,1)}, bf16[64,6144]{1,0:T(8,128)(2,1)}, f32[256,128]{1,0:T(8,128)}, bf16[64,6144]{1,0:T(8,128)(2,1)}) custom-call(bf16[128,6144]{1,0:T(8,128)(2,1)} %bitcast.18, bf16[128,6144]{1,0:T(8,128)(2,1)} %bitcast.19, bf16[128,6144]{1,0:T(8,128)(2,1)} %bitcast.20, bf16[128,6144]{1,0:T(8,128)(2,1)} %bitcast.21, ...), custom_call_target="tpu_custom_call" | custom-call | tf_op jit(solution)/shard_map/layer/pallas_call | solution.py:648
  129.1 0.0 copy-start
  129.1 1.4 %copy-done = bf16[128,6144]{1,0:T(8,128)(2,1)S(1)} copy-done((bf16[128,6144]{1,0:T(8,128)(2,1)S(1)}, bf16[128,6144]{1,0:T(8,128)(2,1)}, u32[]{:S(2)}) %copy-start) | copy-done | bytes 1572888
  130.5 0.0 copy-start.1
  130.5 1.1 copy-done.1
  131.7 0.0 copy-start.2
  131.7 1.1 copy-done.2
  132.8 0.0 copy-start.3
  132.8 0.9 copy-done.3
  133.7 2.6 %mix.1 = bf16[128,6144]{1,0:T(8,128)(2,1)} custom-call(bf16[128,6144]{1,0:T(8,128)(2,1)S(1)} %copy-done, bf16[64,6144]{1,0:T(8,128)(2,1)S(1)} %copy-done.1, f32[256,128]{1,0:T(8,128)S(1)} %copy-done.3, bf16[64,6144]{1,0:T(8,128)(2,1)S(1)} %copy-done.2), custom_call_target="tpu_custom_call" | custom-call | tf_op jit(solution)/shard_map/mix/pallas_call | solution.py:700
Async XLA Ops:
  129.1 1.4 %copy-start = (bf16[128,6144]{1,0:T(8,128)(2,1)S(1)}, bf16[128,6144]{1,0:T(8,128)(2,1)}, u32[]{:S(2)}) copy-start(bf16[128,6144]{1,0:T(8,128)(2,1)} %get-tuple-element.9.high_ref) | copy-start | bytes 4718596
  130.5 1.1 copy-start.1
  131.7 1.1 copy-start.2
  132.8 0.9 copy-start.3

commit v6 on v5

--- a/solution.py
+++ b/solution.py
@@ -11,7 +11,9 @@
 TOK = 128
 CAP = 16
 FLY = 4
+GROUPS = 3
 SUB = 2
+BATCH = 4 * SUB
 ROWS = SUB * HEAD
 MESSAGE = ROWS + 8
 BF = jnp.bfloat16
@@ -57,12 +59,12 @@
 def scan_attention(
     where, barrier,
     q_hbm, k_hbm, v_hbm, resid_hbm, rate_ref, attn_gain_ref, moe_gain_ref, experts_ref, combine_ref,
-    high_ref, low_ref, outbox_ref, mixing_ref,
+    attn_ref, first_ref, weight_ref, outbox_ref, mixing_ref,
     partner_total, partner_state, t_recv, r_recv, chip_prefix, prefix,
     load_sems, small_sems, ps_send_sems, ps_recv_sems, t_send_sems, t_recv_sems,
     r_send_sems, r_recv_sems, p_send_sems, p_recv_sems, f_send_sems, f_recv_sems,
     q_ref, k_ref, v_ref, resid_ref, cum_ref, total_ref, own_state,
-    t_send, within, r_send, p_send, f_send, attn_ref, square_ref, select_ref,
+    t_send, within, r_send, p_send, f_send, square_ref, select_ref,
 ):
     y, z, c = where
     loads = [
@@ -107,10 +109,10 @@
 
     def states(half, s):
         def one(n, carry):
-            own_state[half, s, tile(n), :] = state_of(half * 24 + s * 8 + n)
+            own_state[half, s, tile(n), :] = state_of(half * 24 + s * BATCH + n)
             return carry
 
-        lax.fori_loop(0, 8, one, 0, unroll=8)
+        lax.fori_loop(0, BATCH, one, 0, unroll=BATCH)
 
     loads[0].wait()
     loads[1].wait()
@@ -132,7 +134,7 @@
             j = lax.rem(z + d, 4)
             target = t_recv.at[s, 0] if d == 0 else t_send.at[s, d - 1]
             for i in range(SUB):
-                h = c * 24 + s * 8 + j * SUB + i
+                h = c * 24 + s * BATCH + j * SUB + i
                 rows = tile(j * SUB + i)
                 mine = total_ref[pl.ds(h, 1), :]
                 other = partner_total[pl.ds(h, 1), :]
@@ -228,7 +230,7 @@
                 p_copies[s, d].wait_recv()
             j = lax.rem(z - d + 4, 4)
             for i in range(SUB):
-                h = c * 24 + s * 8 + j * SUB + i
+                h = c * 24 + s * BATCH + j * SUB + i
                 rows = tile(j * SUB + i)
                 first_total = jnp.where(
                     zero_first, total_ref[pl.ds(h, 1), :], partner_total[pl.ds(h, 1), :]
@@ -255,13 +257,15 @@
         match = either & (ahead == slot.astype(F32))
         found = match.astype(F32)
         select_ref[...] = found.T[: FLY * CAP, :].astype(BF)
-        first = jnp.where(chosen[0] < FLY, named[0].astype(F32), named[1].astype(F32))
-        mixing_ref[:TOK, :] = first * found
-        mixing_ref[TOK:, :] = jnp.where(named[0], weight[0], weight[1]) * found
+        first = jnp.where(chosen[0] < FLY, named[0].astype(F32), named[1].astype(F32)) * found
+        first_ref[...] = first.T[: FLY * CAP, :].astype(BF)
+        mixing_ref[...] = found.astype(BF)
+        weighted = (jnp.where(named[0], weight[0], weight[1]) * found).T[: FLY * CAP, :]
+        weight_ref[...] = jnp.broadcast_to(jnp.sum(weighted, axis=1, keepdims=True), (FLY * CAP, TOK))
 
     def inter(half, s):
         def one(n, carry):
-            h = half * 24 + s * 8 + n
+            h = half * 24 + s * BATCH + n
             across = jnp.broadcast_to(cum_ref[pl.ds(h, 1), :], (TOK, TOK)).T
             high, low = parts(prefix[half, s, tile(n), :])
             query = q_ref[:, columns(h)]
@@ -270,14 +274,14 @@
             square_ref[...] += out * out
             return carry
 
-        lax.fori_loop(0, 8, one, 0, unroll=8)
+        lax.fori_loop(0, BATCH, one, 0, unroll=BATCH)
 
     swaps = [swap(0)]
     states(c, 0)
     totals.wait_recv()
     swaps[0].wait_recv()
     join(0)
-    for s in (1, 2):
+    for s in range(1, GROUPS):
         states(1 - c, s)
         swaps.append(swap(s))
         states(c, s)
@@ -295,7 +299,7 @@
     chip_prefixes(1)
     intra(36, 48)
     chip_prefixes(2)
-    for s in range(3):
+    for s in range(GROUPS):
         finish(s)
         inter(c, s)
         f_copies[s].wait_recv()
@@ -318,9 +322,6 @@
 
     def norm(h, carry):
         out = attn_ref[:, columns(h)]
-        high, low = parts(out)
-        high_ref[:, columns(h)] = high
-        low_ref[:, columns(h)] = dot(select, low).astype(BF)
         normed = (out * scale_2 * moe_gain_ref[:, columns(h)]).astype(BF)
         outbox_ref[:, columns(h)] = dot(select, normed).astype(BF)
         return carry
@@ -332,11 +333,12 @@
 
 def expert_window(
     where,
-    outbox_ref, high_ref, low_ref, mixing_ref, up_hbm, down_hbm,
-    high_in, low_in, mixing_in, sums_ref,
+    attn_ref, first_ref, weight_ref, outbox_ref, high_ref, low_ref, mixing_ref,
+    up_hbm, down_hbm, high_in, low_in, weight_in, mixing_in, sums_ref,
     rows_ref, partner_part, relay_in, near_in, far_in,
     load_sems, y_send, y_recv, core_send, core_recv, z_send, z_recv, hop_send, hop_recv,
     part_send, part_recv, ring_send, ring_recv, next_send, next_recv, sums_send, sums_recv,
+    low_send, low_recv, weight_send, weight_recv,
     up_ref, down_ref, total_ref, hidden_ref, part_ref, sum_ref, relay_out, final_ref,
 ):
     y, z, c = where
@@ -500,14 +502,22 @@
             mine = share(g, q, 0, i)
             p = 2 * g + i
 
-            def add(at, i=i, p=p, mine=mine):
-                final_ref[q, p * CAP : (p + 1) * CAP, at] = (
+            weight = jnp.concatenate([weight_in[p]] * (NARROW // TOK), axis=1)
+
+            def add(n, carry, i=i, p=p, mine=mine, weight=weight):
+                at = pl.ds(pl.multiple_of(n * NARROW, NARROW), NARROW)
+                low_at = pl.ds(pl.multiple_of(q * WIDE + n * NARROW, NARROW), NARROW)
+                total = (
                     mine[:, at].astype(F32)
                     + near_in[g, q, 1 - i, :, at].astype(F32)
                     + far_in[g, q, i, :, at].astype(F32)
+                )
+                final_ref[q, p * CAP : (p + 1) * CAP, at] = (
+                    total * weight + low_in[p, :, low_at].astype(F32)
                 ).astype(BF)
-
-            over_columns(add)
+                return carry
+
+            lax.fori_loop(0, WIDE // NARROW, add, 0)
             d = spot[p]
             send(
                 final_ref.at[q, p * CAP : (p + 1) * CAP, :], sums_ref.at[box(y), q * WIDE : (q + 1) * WIDE],
@@ -515,15 +525,31 @@
             )
 
     spread(0)
+
+    def split(h, carry):
+        high, low = parts(attn_ref[:, columns(h)])
+        high_ref[:, columns(h)] = high
+        low_ref[:, columns(h)] = dot(first_ref[...], low).astype(BF)
+        return carry
+
+    lax.fori_loop(0, HEADS, split, 0, unroll=6)
     send(high_ref, high_in, next_send.at[0], next_recv.at[0], y_peer[0], after)
-    send(low_ref, low_in, next_send.at[1], next_recv.at[1], y_peer[0], after)
-    send(mixing_ref, mixing_in, next_send.at[2], next_recv.at[2], y_peer[0], after)
+    send(mixing_ref, mixing_in, next_send.at[1], next_recv.at[1], y_peer[0], after)
     from_column(1)
     to_column(2)
     from_column(3)
     from_minus(0)
     from_plus(0)
     from_column(2)
+    low_in[0] = low_ref[box(y), :]
+    weight_in[0] = weight_ref[box(y), :]
+    for d in (1, 3, 2):
+        e = box(lax.rem(y + d, 4))
+        send(low_ref.at[e, :], low_in.at[spot[d]], low_send.at[d - 1], low_recv.at[d - 1], y_peer[d])
+        send(
+            weight_ref.at[e, :], weight_in.at[spot[d]],
+            weight_send.at[d - 1], weight_recv.at[d - 1], y_peer[d],
+        )
     from_minus(1)
     from_plus(1)
     from_far(0)
@@ -545,6 +571,9 @@
     up(1)
     for q in range(CHUNKS):
         relay(0, q)
+    for d in (1, 3, 2):
+        arrived(low_in.at[spot[d]], low_recv.at[d - 1], y_peer[4 - d])
+        arrived(weight_in.at[spot[d]], weight_recv.at[d - 1], y_peer[4 - d])
     down(1, 0)
     down(1, 1)
     core_sum(1, 0)
@@ -559,8 +588,7 @@
     final(1, 0)
     relay(1, 2)
     arrived(high_in, next_recv.at[0], y_peer[0], before)
-    arrived(low_in, next_recv.at[1], y_peer[0], before)
-    arrived(mixing_in, next_recv.at[2], y_peer[0], before)
+    arrived(mixing_in, next_recv.at[1], y_peer[0], before)
     final(1, 1)
     final(1, 2)
     for q in range(CHUNKS):
@@ -573,8 +601,8 @@
 def layer_kernel(
     q_hbm, k_hbm, v_hbm, resid_hbm, rate_ref, attn_gain_ref, moe_gain_ref, experts_ref, combine_ref,
     up_hbm, down_hbm,
-    high_in, low_in, mixing_in, sums_ref,
-    high_ref, low_ref, outbox_ref, mixing_ref,
+    high_in, mixing_in, sums_ref,
+    attn_ref, first_ref, weight_ref, high_ref, low_ref, outbox_ref, mixing_ref, low_in, weight_in,
     partner_total, partner_state, t_recv, r_recv, chip_prefix, prefix,
     rows_ref, partner_part, relay_in, near_in, far_in,
     *sems,
@@ -596,7 +624,7 @@
         scan_attention(
             (y, z, c), barrier,
             q_hbm, k_hbm, v_hbm, resid_hbm, rate_ref, attn_gain_ref, moe_gain_ref, experts_ref, combine_ref,
-            high_ref, low_ref, outbox_ref, mixing_ref,
+            attn_ref, first_ref, weight_ref, outbox_ref, mixing_ref,
             partner_total, partner_state, t_recv, r_recv, chip_prefix, prefix,
             *sems[:12], *local_refs,
         )
@@ -609,21 +637,20 @@
         pltpu.VMEM((TOK, D), BF),
         pltpu.VMEM((HEADS, TOK), F32),
         pltpu.VMEM((HEADS, TOK), F32),
-        pltpu.VMEM((2, 3, 4 * ROWS, HEAD), F32),
-        pltpu.VMEM((3, 3, MESSAGE, HEAD), F32),
-        pltpu.VMEM((3, 4, ROWS, HEAD), F32),
-        pltpu.VMEM((3, MESSAGE, HEAD), F32),
-        pltpu.VMEM((3, 3, ROWS, HEAD), F32),
-        pltpu.VMEM((3, 4 * ROWS, HEAD), F32),
-        pltpu.VMEM((TOK, D), F32),
+        pltpu.VMEM((2, GROUPS, 4 * ROWS, HEAD), F32),
+        pltpu.VMEM((GROUPS, 3, MESSAGE, HEAD), F32),
+        pltpu.VMEM((GROUPS, 4, ROWS, HEAD), F32),
+        pltpu.VMEM((GROUPS, MESSAGE, HEAD), F32),
+        pltpu.VMEM((GROUPS, 3, ROWS, HEAD), F32),
+        pltpu.VMEM((GROUPS, 4 * ROWS, HEAD), F32),
         pltpu.VMEM((TOK, HEAD), F32),
         pltpu.VMEM((FLY * CAP, TOK), BF),
     )
 
     def second(*local_refs):
         expert_window(
-            (y, z, c), outbox_ref, high_ref, low_ref, mixing_ref, up_hbm, down_hbm,
-            high_in, low_in, mixing_in, sums_ref,
+            (y, z, c), attn_ref, first_ref, weight_ref, outbox_ref, high_ref, low_ref, mixing_ref,
+            up_hbm, down_hbm, high_in, low_in, weight_in, mixing_in, sums_ref,
             rows_ref, partner_part, relay_in, near_in, far_in,
             *sems[12:], *local_refs,
         )
@@ -649,34 +676,40 @@
         layer_kernel,
         out_shape=(
             jax.ShapeDtypeStruct((TOK, D), BF),
-            jax.ShapeDtypeStruct((BLOCK, D), BF),
-            jax.ShapeDtypeStruct((2 * TOK, TOK), F32),
+            jax.ShapeDtypeStruct((TOK, TOK), BF),
             jax.ShapeDtypeStruct((BLOCK, D), BF),
         ),
         in_specs=[hbm] * 4 + [vmem] * 5 + [hbm] * 2,
-        out_specs=(hbm, hbm, hbm, hbm),
+        out_specs=(hbm, hbm, hbm),
         scratch_shapes=[
+            pltpu.VMEM((TOK, D), F32),
+            pltpu.VMEM((BLOCK, TOK), BF),
+            pltpu.VMEM((BLOCK, TOK), F32),
             pltpu.VMEM((TOK, D), BF),
             pltpu.VMEM((BLOCK, D), BF),
             pltpu.VMEM((BLOCK, D), BF),
-            pltpu.VMEM((2 * TOK, TOK), F32),
+            pltpu.VMEM((TOK, TOK), BF),
+            pltpu.VMEM((4, CAP, D), BF),
+            pltpu.VMEM((4, CAP, TOK), F32),
             pltpu.VMEM((HEADS, TOK), F32),
-            pltpu.VMEM((3, 4 * ROWS, HEAD), F32),
-            pltpu.VMEM((3, 4, MESSAGE, HEAD), F32),
-            pltpu.VMEM((3, 4, MESSAGE, HEAD), F32),
-            pltpu.VMEM((3, 4, ROWS, HEAD), F32),
-            pltpu.VMEM((2, 3, 4 * ROWS, HEAD), F32),
+            pltpu.VMEM((GROUPS, 4 * ROWS, HEAD), F32),
+            pltpu.VMEM((GROUPS, 4, MESSAGE, HEAD), F32),
+            pltpu.VMEM((GROUPS, 4, MESSAGE, HEAD), F32),
+            pltpu.VMEM((GROUPS, 4, ROWS, HEAD), F32),
+            pltpu.VMEM((2, GROUPS, 4 * ROWS, HEAD), F32),
             pltpu.VMEM((8 * BLOCK, D), BF),
             pltpu.VMEM((2, CHUNKS, 4 * PAIR, WIDE), BF),
             pltpu.VMEM((2, CHUNKS, 2, CAP, WIDE), BF),
             pltpu.VMEM((2, CHUNKS, 2, CAP, WIDE), BF),
             pltpu.VMEM((2, CHUNKS, 2, CAP, WIDE), BF),
-            dma((4,)), dma((2,)), dma((3,)), dma((3,)), dma((3, 3)), dma((3, 3)),
-            dma((3, 3)), dma((3, 3)), dma((3, 3)), dma((3, 3)), dma((3,)), dma((3,)),
+            dma((4,)), dma((2,)), dma((GROUPS,)), dma((GROUPS,)), dma((GROUPS, 3)), dma((GROUPS, 3)),
+            dma((GROUPS, 3)), dma((GROUPS, 3)), dma((GROUPS, 3)), dma((GROUPS, 3)), dma((GROUPS,)),
+            dma((GROUPS,)),
             dma((2,)), dma((3,)), dma((3,)), dma((4, 4)), dma((4, 4)), dma((2, 4)), dma((2, 4)),
             dma((4,)), dma((4,)), dma((2, CHUNKS)), dma((2, CHUNKS)),
             dma((2, CHUNKS, 6)), dma((2, CHUNKS, 6)),
-            dma((3,)), dma((3,)), dma((CHUNKS, 4)), dma((CHUNKS, 4)),
+            dma((2,)), dma((2,)), dma((CHUNKS, 4)), dma((CHUNKS, 4)),
+            dma((3,)), dma((3,)), dma((3,)), dma((3,)),
         ],
         compiler_params=pltpu.CompilerParams(
             collective_id=0, has_side_effects=True, vmem_limit_bytes=60 * 2**20
@@ -685,17 +718,14 @@
     )(queries, keys, values, resid, rate, attn_gain, moe_gain, experts, combine, w_up, w_down)
 
 
-def mix_kernel(high_ref, low_ref, mixing_ref, sums_ref, out_ref):
-    first = mixing_ref[:TOK, :BLOCK].astype(BF)
-    weight_high, weight_low = parts(mixing_ref[TOK:, :BLOCK])
+def mix_kernel(high_ref, mixing_ref, sums_ref, out_ref):
+    mixing = mixing_ref[:, :BLOCK]
     for i in range(D // 2 // NARROW):
         at = slice(i * NARROW, (i + 1) * NARROW)
-        sums = sums_ref[:, at]
-        mixed = dot(weight_high, sums) + dot(weight_low, sums)
-        out_ref[:, at] = ((high_ref[:, at].astype(F32) + dot(first, low_ref[:, at])) + mixed).astype(BF)
-
-
-def mix(high, low, mixing, sums):
+        out_ref[:, at] = (high_ref[:, at].astype(F32) + dot(mixing, sums_ref[:, at])).astype(BF)
+
+
+def mix(high, mixing, sums):
     wide = D // 2
     return pl.pallas_call(
         mix_kernel,
@@ -703,24 +733,23 @@
         grid=(D // wide,),
         in_specs=[
             pl.BlockSpec((TOK, wide), lambda i: (0, i)),
-            pl.BlockSpec((BLOCK, wide), lambda i: (0, i)),
-            pl.BlockSpec((2 * TOK, TOK), lambda i: (0, 0)),
+            pl.BlockSpec((TOK, TOK), lambda i: (0, 0)),
             pl.BlockSpec((BLOCK, wide), lambda i: (0, i)),
         ],
         out_specs=pl.BlockSpec((TOK, wide), lambda i: (0, i)),
-        compiler_params=pltpu.CompilerParams(vmem_limit_bytes=32 * 2**20),
+        compiler_params=pltpu.CompilerParams(vmem_limit_bytes=60 * 2**20),
         name="mix",
-    )(high, low, mixing, sums)
+    )(high, mixing, sums)
 
 
 def local(
     resid, queries, keys, values, log_decay, attn_gain, moe_gain, experts, combine_weight, w_up, w_down
 ):
-    high, low, mixing, sums = layer(
+    high, mixing, sums = layer(
         queries[0], keys[0], values[0], resid[0], log_decay[0].T, attn_gain, moe_gain,
         experts[0].T, combine_weight[0].T, w_up[0], w_down[0],
     )
-    return mix(high, low, mixing, sums)[None]
+    return mix(high, mixing, sums)[None]
 
 
 def solution(mesh):

time: 137 us -> 129 us (0.942)
  local copies, waits for them, and re-layouts: 4.57 us -> 0 us
  Pallas kernels: 132 us -> 128 us
    unnamed x8 -> x0, local copies, waits for them, and re-layouts: 4.57 us -> none
    pallas_call x1, Pallas kernels: 129 us -> 126 us  [layer(): pl.pallas_call(layer_kernel, out_shape=(jax.ShapeDtypeStruct((TOK, D), BF...]
where the time goes in v6:
time: 129 us; the launch traced here: 128 us
  Pallas kernels  128 us (99%)
    pallas_call x1, Pallas kernels, layer(): pl.pallas_call(layer_kernel, out_shape=(jax.ShapeDtypeStruct((TOK, D), BF...  126 us
    pallas_call x1, Pallas kernels, mix(): pl.pallas_call(mix_kernel, out_shape=jax.ShapeDtypeStruct((TOK, D), BF),...  2.85 us

profile of v6, /device:TPU:0, one launch (start us, length us, event | category | flops | bytes accessed | tf_op | source)
XLA Modules:
  0.0 128.5 jit_solution(3297367978897580337)
XLA Ops:
  0.0 125.6 %layer.1 = (bf16[128,6144]{1,0:T(8,128)(2,1)}, bf16[128,128]{1,0:T(8,128)(2,1)}, bf16[64,6144]{1,0:T(8,128)(2,1)}) custom-call(bf16[128,6144]{1,0:T(8,128)(2,1)} %bitcast.18, bf16[128,6144]{1,0:T(8,128)(2,1)} %bitcast.19, bf16[128,6144]{1,0:T(8,128)(2,1)} %bitcast.20, bf16[128,6144]{1,0:T(8,128)(2,1)} %bitcast.21, f32[48,128]{1,0:T(8,128)} %bitcast.22, ...), custom_call_target="tpu_custom_call" | custom-call | tf_op jit(solution)/shard_map/layer/pallas_call | solution.py:675
  125.6 2.8 %mix.1 = bf16[128,6144]{1,0:T(8,128)(2,1)} custom-call(bf16[128,6144]{1,0:T(8,128)(2,1)} %get-tuple-element.8.high_ref, bf16[128,128]{1,0:T(8,128)(2,1)} %get-tuple-element.9.mixing_ref, bf16[64,6144]{1,0:T(8,128)(2,1)} %get-tuple-element.10.sums_ref), custom_call_target="tpu_custom_call" | custom-call | tf_op jit(solution)/shard_map/mix/pallas_call | solution.py:730

commit v7 on v6

--- a/solution.py
+++ b/solution.py
@@ -462,7 +462,7 @@
         first = block * PAIR + i * CAP
         return sum_ref.at[g, q, first : first + CAP, :]
 
-    def core_sum(g, q):
+    def core_add(g, q):
         arrived(partner_part.at[g, q], part_recv.at[g, q], partner)
 
         def add(at):
@@ -471,11 +471,17 @@
             ).astype(BF)
 
         over_columns(add)
+
+    def ring_out(g, q):
         out, back = ring_send.at[g, q], ring_recv.at[g, q]
         send(share(g, q, 3, 0), relay_in.at[g, q, 0], out.at[2], back.at[2], plus)
         send(share(g, q, 3, 1), relay_in.at[g, q, 1], out.at[3], back.at[3], minus)
         send(share(g, q, 2, 1), near_in.at[g, q, 0], out.at[0], back.at[0], plus)
         send(share(g, q, 1, 0), near_in.at[g, q, 1], out.at[1], back.at[1], minus)
+
+    def core_sum(g, q):
+        core_add(g, q)
+        ring_out(g, q)
 
     def relay(g, q):
         for side in range(2):
@@ -537,10 +543,11 @@
     send(mixing_ref, mixing_in, next_send.at[1], next_recv.at[1], y_peer[0], after)
     from_column(1)
     to_column(2)
-    from_column(3)
     from_minus(0)
     from_plus(0)
-    from_column(2)
+    from_minus(1)
+    from_plus(1)
+    from_column(3)
     low_in[0] = low_ref[box(y), :]
     weight_in[0] = weight_ref[box(y), :]
     for d in (1, 3, 2):
@@ -550,10 +557,9 @@
             weight_ref.at[e, :], weight_in.at[spot[d]],
             weight_send.at[d - 1], weight_recv.at[d - 1], y_peer[d],
         )
-    from_minus(1)
-    from_plus(1)
     from_far(0)
     from_far(1)
+    from_column(2)
     loads[0].wait()
     up(0)
     for p in (2, 3):
@@ -562,12 +568,15 @@
     loads[1].wait()
     down(0, 0)
     down(0, 1)
-    core_sum(0, 0)
+    core_add(0, 0)
     down(0, 2)
-    core_sum(0, 1)
-    core_sum(0, 2)
+    core_add(0, 1)
+    core_add(0, 2)
     from_far(2)
+    ring_out(0, 0)
     from_far(3)
+    ring_out(0, 1)
+    ring_out(0, 2)
     up(1)
     for q in range(CHUNKS):
         relay(0, q)
@@ -578,19 +587,21 @@
     down(1, 1)
     core_sum(1, 0)
     down(1, 2)
-    core_sum(1, 1)
     final(0, 0)
-    core_sum(1, 2)
     final(0, 1)
+    core_add(1, 1)
     relay(1, 0)
+    ring_out(1, 1)
     final(0, 2)
+    core_add(1, 2)
     relay(1, 1)
+    ring_out(1, 2)
     final(1, 0)
     relay(1, 2)
+    final(1, 1)
+    final(1, 2)
     arrived(high_in, next_recv.at[0], y_peer[0], before)
     arrived(mixing_in, next_recv.at[1], y_peer[0], before)
-    final(1, 1)
-    final(1, 2)
     for q in range(CHUNKS):
         for d in range(4):
             arrived(sums_ref.at[0:CAP, q * WIDE : (q + 1) * WIDE], sums_recv.at[q, d], y_peer[d], before)

time: 129 us -> 127 us (0.984)
    pallas_call x1, Pallas kernels: 126 us -> 124 us  [layer(): pl.pallas_call(layer_kernel, out_shape=(jax.ShapeDtypeStruct((TOK, D), BF...]
where the time goes in v7:
time: 127 us
  Pallas kernels  127 us (100%)
    pallas_call x1, Pallas kernels, layer(): pl.pallas_call(layer_kernel, out_shape=(jax.ShapeDtypeStruct((TOK, D), BF...  124 us
    pallas_call x1, Pallas kernels, mix(): pl.pallas_call(mix_kernel, out_shape=jax.ShapeDtypeStruct((TOK, D), BF),...  2.84 us

profile of v7, /device:TPU:0, one launch (start us, length us, event | category | flops | bytes accessed | tf_op | source)
XLA Modules:
  0.0 126.8 jit_solution(836750757133961066)
XLA Ops:
  0.0 123.9 %layer.1 = (bf16[128,6144]{1,0:T(8,128)(2,1)}, bf16[128,128]{1,0:T(8,128)(2,1)}, bf16[64,6144]{1,0:T(8,128)(2,1)}) custom-call(bf16[128,6144]{1,0:T(8,128)(2,1)} %bitcast.18, bf16[128,6144]{1,0:T(8,128)(2,1)} %bitcast.19, bf16[128,6144]{1,0:T(8,128)(2,1)} %bitcast.20, bf16[128,6144]{1,0:T(8,128)(2,1)} %bitcast.21, f32[48,128]{1,0:T(8,128)} %bitcast.22, ...), custom_call_target="tpu_custom_call" | custom-call | tf_op jit(solution)/shard_map/layer/pallas_call | solution.py:686
  124.0 2.8 %mix.1 = bf16[128,6144]{1,0:T(8,128)(2,1)} custom-call(bf16[128,6144]{1,0:T(8,128)(2,1)} %get-tuple-element.8.high_ref, bf16[128,128]{1,0:T(8,128)(2,1)} %get-tuple-element.9.mixing_ref, bf16[64,6144]{1,0:T(8,128)(2,1)} %get-tuple-element.10.sums_ref), custom_call_target="tpu_custom_call" | custom-call | tf_op jit(solution)/shard_map/mix/pallas_call | solution.py:741

commit v8 on v7

--- a/solution.py
+++ b/solution.py
@@ -73,8 +73,8 @@
             ((k_hbm, k_ref), (v_hbm, v_ref), (q_hbm, q_ref), (resid_hbm, resid_ref))
         )
     ]
-    for load in loads:
-        load.start()
+    loads[0].start()
+    loads[1].start()
     partner = index_of(y, z, 1 - c)
     z_peer = [index_of(y, lax.rem(z + d, 4), c) for d in range(4)]
     y_peer = [index_of(lax.rem(y + d, 4), z, c) for d in range(4)]
@@ -116,6 +116,8 @@
 
     loads[0].wait()
     loads[1].wait()
+    loads[2].start()
+    loads[3].start()
     states(1 - c, 0)
     pl.semaphore_wait(barrier, 15)
     totals = remote(total_ref, partner_total, small_sems.at[0], small_sems.at[1], partner)
@@ -297,13 +299,16 @@
     intra(24, 36)
     row_sum(2)
     chip_prefixes(1)
+    chip_prefixes(2)
     intra(36, 48)
-    chip_prefixes(2)
     for s in range(GROUPS):
         finish(s)
         inter(c, s)
-        f_copies[s].wait_recv()
-        inter(1 - c, s)
+        if s:
+            f_copies[s - 1].wait_recv()
+            inter(1 - c, s - 1)
+    f_copies[GROUPS - 1].wait_recv()
+    inter(1 - c, GROUPS - 1)
     loads[3].wait()
     scale = lax.rsqrt(jnp.sum(square_ref[...], axis=1, keepdims=True) * (1.0 / D) + 1e-6)
     scale = jnp.broadcast_to(scale, (TOK, HEAD))
@@ -315,7 +320,7 @@
         square_ref[...] += out * out
         return carry
 
-    lax.fori_loop(0, HEADS, residual, 0, unroll=6)
+    lax.fori_loop(0, HEADS, residual, 0, unroll=12)
     scale_2 = lax.rsqrt(jnp.sum(square_ref[...], axis=1, keepdims=True) * (1.0 / D) + 1e-6)
     scale_2 = jnp.broadcast_to(scale_2, (TOK, HEAD))
     select = select_ref[...]
@@ -326,7 +331,7 @@
         outbox_ref[:, columns(h)] = dot(select, normed).astype(BF)
         return carry
 
-    lax.fori_loop(0, HEADS, norm, 0, unroll=6)
+    lax.fori_loop(0, HEADS, norm, 0, unroll=12)
     for copy in copies:
         copy.wait_send()
 

time: 127 us -> 127 us (level)
  no operation moved by 1% of the time
where the time goes in v8:
time: 127 us; the launch traced here: 126 us
  Pallas kernels  126 us (99%)
    pallas_call x1, Pallas kernels, layer(): pl.pallas_call(layer_kernel, out_shape=(jax.ShapeDtypeStruct((TOK, D), BF...  124 us
    pallas_call x1, Pallas kernels, mix(): pl.pallas_call(mix_kernel, out_shape=jax.ShapeDtypeStruct((TOK, D), BF),...  2.85 us

profile of v8, /device:TPU:0, one launch (start us, length us, event | category | flops | bytes accessed | tf_op | source)
XLA Modules:
  0.0 126.5 jit_solution(4704859101868953621)
XLA Ops:
  0.0 123.6 %layer.1 = (bf16[128,6144]{1,0:T(8,128)(2,1)}, bf16[128,128]{1,0:T(8,128)(2,1)}, bf16[64,6144]{1,0:T(8,128)(2,1)}) custom-call(bf16[128,6144]{1,0:T(8,128)(2,1)} %bitcast.18, bf16[128,6144]{1,0:T(8,128)(2,1)} %bitcast.19, bf16[128,6144]{1,0:T(8,128)(2,1)} %bitcast.20, bf16[128,6144]{1,0:T(8,128)(2,1)} %bitcast.21, f32[48,128]{1,0:T(8,128)} %bitcast.22, ...), custom_call_target="tpu_custom_call" | custom-call | tf_op jit(solution)/shard_map/layer/pallas_call | solution.py:691
  123.6 2.8 %mix.1 = bf16[128,6144]{1,0:T(8,128)(2,1)} custom-call(bf16[128,6144]{1,0:T(8,128)(2,1)} %get-tuple-element.8.high_ref, bf16[128,128]{1,0:T(8,128)(2,1)} %get-tuple-element.9.mixing_ref, bf16[64,6144]{1,0:T(8,128)(2,1)} %get-tuple-element.10.sums_ref), custom_call_target="tpu_custom_call" | custom-call | tf_op jit(solution)/shard_map/mix/pallas_call | solution.py:746
